TPU v7x, 512 devices: a whole 4x4x16 slice. The times are simulated.
512 devices in a mesh: param: 16 (over y, x), dom: 32 (over z, core).
Axes of the slice: x: 4, y: 4, z: 16, core: 2. Of those that a mesh axis runs over, the one named last changes fastest.
Arguments:
- particles: bfloat16 [512, 524288], P('dom', 'param'), may hold values from -40 to 40
- scores: bfloat16 [512, 524288], P('dom', 'param'), may hold values from -6 to 6
- basis: bfloat16 [524288, 128], P(('param', 'dom')), may hold values from -0.0078125 to 0.0078125
Outputs:
- velocity: bfloat16 [512, 524288], P('dom', 'param')
- phi: float32 [512, 128], P('dom')
All inputs are finite; a program needn't handle non-finite values.
Results may differ from a plain program's by a relative error of at most 0.0049.
Values may be sent and summed in bfloat16 or wider, within the bound.
No kernel may reach another device: no remote copies, remote signals or barrier semaphores. Data moves between devices by JAX's collectives and lax.ppermute only.
A program may use at most 64 MiB of HBM per device.

v0:
```python
import math

import jax
import jax.numpy as jnp
from jax import lax
from jax.sharding import PartitionSpec as P

P_SIZE = 524288
R = 128


def sent_to_all(array, axis):
    peers = lax.axis_size(axis)
    return lax.all_to_all(
        jnp.broadcast_to(array[None], (peers, *array.shape)), axis, 0, 0, tiled=True
    )


def of_everyone(array, axis):
    return sent_to_all(array, axis).sum(axis=0)


def in_one(arrays, axis):
    ends = [0]
    for a in arrays:
        ends.append(ends[-1] + a.size)
    total = of_everyone(jnp.concatenate([a.ravel() for a in arrays]), axis)
    return tuple((total[b:e].reshape(a.shape) for a, b, e in zip(arrays, ends, ends[1:])))


def in_one_piece(arrays, axis, dim, along):
    widths = [a.shape[along] for a in arrays]
    both = jnp.concatenate(arrays, axis=along)
    result = lax.all_gather(both, axis, axis=dim, tiled=True)
    return tuple(jnp.split(result, [sum(widths[:k]) for k in range(1, len(widths))], axis=along))


def stein_terms(own, every, every_score):
    count = every.shape[0]
    every_sq = jnp.sum(every * every, axis=1)
    own_sq = jnp.sum(own * own, axis=1)
    center = jnp.mean(every, axis=0)
    width = 2.0 * (jnp.mean(every_sq) - jnp.sum(center * center)) / math.log(count) + 1e-06
    cross = jnp.dot(own, every.T, precision=lax.Precision.HIGHEST)
    dist = own_sq[:, None] + every_sq[None, :] - 2.0 * cross
    kern = jnp.exp(-dist / width)
    drive = jnp.dot(kern, every_score, precision=lax.Precision.HIGHEST)
    pull = jnp.dot(kern, every, precision=lax.Precision.HIGHEST)
    total = jnp.sum(kern, axis=1)
    return (drive + 2.0 / width * (own * total[:, None] - pull)) / count


def lift_rows(phi_rows, basis_rows):
    lifted = lax.dot_general(
        phi_rows.astype(jnp.bfloat16),
        basis_rows,
        (((1,), (1,)), ((), ())),
        preferred_element_type=jnp.float32,
    )
    return (lifted * math.sqrt(P_SIZE / R)).astype(jnp.bfloat16)


def body(particles, scores, basis):
    rows = particles.shape[0]
    first = lax.axis_index("dom") * rows
    block_basis = lax.all_gather(basis, "dom", axis=0, tiled=True)
    partial_c = jnp.dot(particles, block_basis, preferred_element_type=jnp.float32)
    partial_s = jnp.dot(scores, block_basis, preferred_element_type=jnp.float32)
    summed_c, summed_s = in_one((partial_c, partial_s), "param")
    every, every_score = in_one_piece((summed_c, summed_s), "dom", 0, 1)
    own = lax.dynamic_slice_in_dim(every, first, rows, 0)
    phi = stein_terms(own, every, every_score)
    velocity = lift_rows(phi, block_basis)
    return (velocity, phi)


def solution(mesh):
    in_specs = (P("dom", "param"), P("dom", "param"), P(("param", "dom"), None))
    out_specs = (P("dom", "param"), P("dom", None))
    return jax.shard_map(body, mesh=mesh, in_specs=in_specs, out_specs=out_specs, check_vma=False)
```

profile of v0, /device:TPU:1, one launch (start us, length us, event | category | flops | bytes accessed | tf_op | source)
XLA Modules:
  0.0 167.6 jit_solution(8513275402666287345)
XLA Ops:
  7.2 0.0 copy-start
  7.2 0.0 all-gather.2.cloned.1.call-start
  7.2 0.7 all-gather.2.cloned.1.call-update
  7.9 0.0 copy-start.2
  7.9 87.5 %all-gather.2.cloned.1.call-done = bf16[32768,128]{1,0:T(8,128)(2,1)} async-done(((bf16[1024,128]{1,0:T(8,128)(2,1)}), bf16[32768,128]{1,0:T(8,128)(2,1)}) %all-gather.2.cloned.1.call-update) | async-done | bytes 8388624 | tf_op jit(solution)/shard_map/all_gather | solution.py:66
  95.4 0.0 copy-done
  95.4 0.0 copy-start.1
  95.4 4.7 %convolution_bitcast_fusion = f32[2048]{0:T(1024)S(1)} fusion(bf16[16,32768]{1,0:T(8,128)(2,1)S(1)} %copy-done, bf16[32768,128]{1,0:T(8,128)(2,1)} %all-gather.2.cloned.1.call-done), kind=kOutput, calls=%fused_computation.11 | convolution fusion | flops 134217728 | bytes 9445376 | tf_op jit(solution)/shard_map/dot_general | solution.py:68
  100.2 0.0 copy-done.2
  100.2 1.0 copy-done.1
  101.2 1.3 convolution_bitcast_fusion.1
  102.5 0.9 broadcast_in_dim.2
  103.4 6.5 %all-to-all-start = ((f32[16,1,4096]{2,1,0:T(1,128)}), f32[16,1,4096]{2,1,0:T(1,128)S(1)}, u32[]{:S(2)}, u32[]{:S(2)}) async-start(f32[16,1,4096]{2,1,0:T(1,128)} %broadcast_in_dim.2), calls=%async_computation | async-start | bytes 524288 | tf_op jit(solution)/shard_map/all_to_all | solution.py:14
  109.9 8.2 %all-to-all-done = f32[16,1,4096]{2,1,0:T(1,128)S(1)} async-done(((f32[16,1,4096]{2,1,0:T(1,128)}), f32[16,1,4096]{2,1,0:T(1,128)S(1)}, u32[]{:S(2)}, u32[]{:S(2)}) %all-to-all-start) | async-done | bytes 262176 | tf_op jit(solution)/shard_map/all_to_all | solution.py:14
  118.2 0.2 reduce_sum.63
  118.4 32.0 %all_gather.7 = f32[512,256]{1,0:T(8,128)S(1)} all-gather(f32[16,256]{1,0:T(8,128)S(1)} %pad_maximum_fusion.1), channel_id=1, replica_groups=mesh['param'=16,'dom'=32] {'dom'}, dimensions={0}, use_global_device_ids=true | all-gather | bytes 540672 | tf_op jit(solution)/shard_map/all_gather | solution.py:34
  150.4 0.7 multiply_reduce_fusion.1
  151.1 0.6 multiply_reduce_fusion.3
  153.0 0.1 multiply_reduce_fusion.2
  153.2 0.4 fusion.13
  153.6 0.2 fusion.8
  153.9 0.2 fusion.7
  154.1 0.0 copy-start.3
  154.1 6.7 %fusion = bf16[16,32768]{1,0:T(8,128)(2,1)} fusion(bf16[32768,128]{1,0:T(8,128)(2,1)} %all-gather.2.cloned.1.call-done, f32[16,128]{1,0:T(8,128)S(1)} %fusion.7), kind=kOutput, calls=%fused_computation.1 | convolution fusion | flops 135268352 | bytes 9445376 | tf_op jit(solution)/shard_map/dot_general | solution.py:54
  160.8 0.0 copy-done.3
  (3 shorter events, 0.0 us)
Async XLA Ops:
  7.2 88.3 %copy-start = (bf16[16,32768]{1,0:T(8,128)(2,1)S(1)}, bf16[16,32768]{1,0:T(8,128)(2,1)}, u32[]{:S(2)}) copy-start(bf16[16,32768]{1,0:T(8,128)(2,1)} %param.4) | copy-start | bytes 3145732
  7.2 88.3 %all-gather.2.cloned.1.call-start = ((), (), s32[]{:S(2)}) async-start(), calls=%async_computation.1 | async-start | bytes 8650752 | tf_op jit(solution)/shard_map/all_gather | solution.py:66
  7.9 92.3 %copy-start.2 = (bf16[16,32768]{1,0:T(8,128)(2,1)S(1)}, bf16[16,32768]{1,0:T(8,128)(2,1)}, u32[]{:S(2)}) copy-start(bf16[16,32768]{1,0:T(8,128)(2,1)} %param.3) | copy-start | bytes 3145732
  95.4 5.8 %copy-start.1 = (bf16[32768,128]{1,0:T(8,128)(2,1)S(1)}, bf16[32768,128]{1,0:T(8,128)(2,1)}, u32[]{:S(2)}) copy-start(bf16[32768,128]{1,0:T(8,128)(2,1)} %all-gather.2.cloned.1.call-done) | copy-start | bytes 25165828
  103.4 14.8 %all-to-all-start = ((f32[16,1,4096]{2,1,0:T(1,128)}), f32[16,1,4096]{2,1,0:T(1,128)S(1)}, u32[]{:S(2)}, u32[]{:S(2)}) async-start(f32[16,1,4096]{2,1,0:T(1,128)} %broadcast_in_dim.2), calls=%async_computation | async-start | bytes 524288 | tf_op jit(solution)/shard_map/all_to_all | solution.py:14
  154.1 6.7 %copy-start.3 = (f32[16,128]{1,0:T(8,128)}, f32[16,128]{1,0:T(8,128)S(1)}, u32[]{:S(2)}) copy-start(f32[16,128]{1,0:T(8,128)S(1)} %fusion.7) | copy-start | bytes 24580
Sparse Core Ops, SparseCore 0:
  10.1 85.2 all-gather.1
where the time goes:
time: 168 us
  waiting for transfers between devices  96.4 us (57%)
  blocking collectives  32 us (19%)
  between operations  15.5 us (9%)
  matrix products  13.6 us (8%)
  starting transfers between devices  6.57 us (4%)
  local copies, waits for them, and re-layouts  1.96 us (1%)
    all_gather x1, waiting for transfers between devices, body(): block_basis = lax.all_gather(basis, 'dom', axis=0, tiled=True)  87.5 us
    all_gather x1, blocking collectives, in_one_piece(): result = lax.all_gather(both, axis, axis=dim, tiled=True)  32 us
    all_to_all x1, waiting for transfers between devices, sent_to_all(): lax.all_to_all(jnp.broadcast_to(array[None], (peers, *array.shape)), axis...  8.23 us
    dot_general x1, matrix products, lift_rows(): lax.dot_general(phi_rows.astype(jnp.bfloat16), basis_rows, (((1,), (1,)),...  6.65 us
    all_to_all x1, starting transfers between devices, sent_to_all(): lax.all_to_all(jnp.broadcast_to(array[None], (peers, *array.shape)), axis...  6.54 us
    dot_general x1, matrix products, body(): partial_s = jnp.dot(scores, block_basis, preferred_element_type=jnp.float32)  4.73 us
  transfers between devices with their start and end apart: 2, of which 2 were waited for; matrix products, arithmetic and copies ran while one was open for 0% of the time, Pallas kernels for 0%

commit v1 on v0

v1 whole, which is shorter than its diff:
```python
import math

import jax
import jax.numpy as jnp
from jax import lax
from jax.sharding import Mesh, PartitionSpec as P

P_SIZE = 524288
R = 128
TAIL = 16
TOP = 15.0


def swap_cores(array):
    return lax.ppermute(array, "core", [(0, 1), (1, 0)])


def packed_shard(basis):
    wide = basis.astype(jnp.float32)
    largest = jnp.maximum(jnp.max(jnp.abs(wide)), 1e-30)
    power = jnp.ceil(jnp.log2(largest))
    scaled = (wide * jnp.exp2(TOP - power)).astype(jnp.float16)
    tail = jnp.full((TAIL, basis.shape[1]), power, jnp.float32).astype(jnp.float16)
    return jnp.concatenate([scaled, tail], axis=0)


def unpacked(gathered, shards):
    rows = gathered.reshape(shards, -1, gathered.shape[1])
    power = rows[:, -TAIL:, :].astype(jnp.float32)[:, :1, :1]
    wide = rows[:, :-TAIL, :].astype(jnp.float32) * jnp.exp2(power - TOP)
    return wide.astype(jnp.bfloat16)


def stein_terms(own, every, every_score):
    count = every.shape[0]
    every_sq = jnp.sum(every * every, axis=1)
    own_sq = jnp.sum(own * own, axis=1)
    center = jnp.mean(every, axis=0)
    width = 2.0 * (jnp.mean(every_sq) - jnp.sum(center * center)) / math.log(count) + 1e-06
    cross = jnp.dot(own, every.T, precision=lax.Precision.HIGHEST)
    dist = own_sq[:, None] + every_sq[None, :] - 2.0 * cross
    kern = jnp.exp(-dist / width)
    drive = jnp.dot(kern, every_score, precision=lax.Precision.HIGHEST)
    pull = jnp.dot(kern, every, precision=lax.Precision.HIGHEST)
    total = jnp.sum(kern, axis=1)
    return (drive + 2.0 / width * (own * total[:, None] - pull)) / count


def sent_to_all(array, axis):
    peers = lax.axis_size(axis)
    return lax.all_to_all(
        jnp.broadcast_to(array[None], (peers, *array.shape)), axis, 0, 0, tiled=True
    )


def contract(rows, half_basis):
    return lax.dot_general(
        rows, half_basis, (((1, 2), (0, 1)), ((), ())), preferred_element_type=jnp.float32
    )


def lift(phi_low, half_basis):
    lifted = lax.dot_general(
        phi_low, half_basis, (((1,), (2,)), ((), ())), preferred_element_type=jnp.float32
    )
    return (lifted * math.sqrt(P_SIZE / R)).astype(jnp.bfloat16)


def body(particles, scores, basis):
    rows = particles.shape[0]
    depth = basis.shape[0]
    shards = lax.axis_size("z")
    core = lax.axis_index("core")
    both = jnp.concatenate([particles, scores], axis=0).reshape(2 * rows, shards, 2, depth)
    theirs = lax.dynamic_index_in_dim(both, 1 - core, 2, keepdims=False)
    mine = lax.dynamic_index_in_dim(both, core, 2, keepdims=False)
    others = swap_cores(theirs)
    gathered = lax.all_gather(packed_shard(basis), "z", axis=0, tiled=True)
    half = unpacked(gathered, shards)
    other_half = swap_cores(half)
    own_part = contract(mine, half)
    other_part = contract(others, half)
    own_part = jnp.concatenate([own_part[:rows], own_part[rows:]], axis=1)
    other_part = jnp.concatenate([other_part[:rows], other_part[rows:]], axis=1)
    first = jnp.where(core == 0, own_part, other_part)
    second = jnp.where(core == 0, other_part, own_part)
    pair = jnp.stack([first, second])
    peers = lax.axis_size("param")
    pieces = jnp.broadcast_to(pair[None], (peers, *pair.shape)).reshape(2 * peers, rows, -1)
    summed = lax.all_to_all(pieces, ("param", "core"), 0, 0, tiled=True).sum(axis=0)
    column = sent_to_all(summed, "z").reshape(shards * rows, -1)
    everyone = lax.all_gather(column, "core", axis=0, tiled=True)
    phi = stein_terms(summed[:, :R], everyone[:, :R], everyone[:, R:])
    phi_low = phi.astype(jnp.bfloat16)
    ours = lift(phi_low, half)
    rest = lift(phi_low, other_half)
    low = jnp.where(core == 0, ours, rest)
    high = jnp.where(core == 0, rest, ours)
    velocity = jnp.stack([low, high], axis=2).reshape(particles.shape)
    return (velocity, phi)


def solution(mesh):
    inner = Mesh(mesh.devices.reshape(mesh.devices.shape[0], -1, 2), ("param", "z", "core"))
    dom = ("z", "core")
    in_specs = (P(dom, "param"), P(dom, "param"), P(("param", "z", "core"), None))
    out_specs = (P(dom, "param"), P(dom, None))
    return jax.shard_map(body, mesh=inner, in_specs=in_specs, out_specs=out_specs, check_vma=False)
```

time: 168 us -> 164 us (0.976)
  waiting for transfers between devices: 96.4 us -> 13.7 us
  blocking collectives: 32 us -> 82 us
  starting transfers between devices: 6.57 us -> 23.7 us
  local copies, waits for them, and re-layouts: 1.96 us -> 15.8 us
  between operations: 15.5 us -> 2.92 us
  other arithmetic: 1.58 us -> 10.8 us
    all_gather x1 -> x0, waiting for transfers between devices: 87.5 us -> none  [body(): block_basis = lax.all_gather(basis, 'dom', axis=0, tiled=True)]
    all_gather x1 -> x2, blocking collectives: 32 us -> 63.5 us  [the longest x1 56.2 us: body(): gathered = lax.all_gather(packed_shard(basis), 'z', axis=0, tiled=True)]
    all_to_all x0 -> x1, blocking collectives: none -> 18.5 us  [body(): lax.all_to_all(pieces, ('param', 'core'), 0, 0, tiled=True).sum(axis=0)]
    ppermute x0 -> x2, starting transfers between devices: none -> 16.6 us  [swap_cores(): return lax.ppermute(array, 'core', [(0, 1), (1, 0)])]
    dynamic_slice x0 -> x1, local copies, waits for them, and re-layouts: none -> 5.76 us  [body(): mine = lax.dynamic_index_in_dim(both, core, 2, keepdims=False)]
    convert_element_type x0 -> x2, other arithmetic: none -> 5.51 us  [the longest x1 5.44 us: unpacked(): return wide.astype(jnp.bfloat16)]
    all_to_all x1, waiting for transfers between devices: 8.23 us -> 13.7 us  [sent_to_all(): lax.all_to_all(jnp.broadcast_to(array[None], (peers, *array.shape)), axis...]
    reshape x0 -> x2, local copies, waits for them, and re-layouts: none -> 4.91 us  [the longest x1 3.3 us: body(): jnp.concatenate([particles, scores], axis=0)]
  transfers between devices with their start and end apart: 2 -> 3, of which waited for: 2 -> 1; matrix products, arithmetic and copies ran while one was open for 0% -> 12% of each run, Pallas kernels for 0% -> 0%
where the time goes in v1:
time: 164 us
  blocking collectives  82 us (50%)
  starting transfers between devices  23.7 us (14%)
  local copies, waits for them, and re-layouts  15.8 us (10%)
  matrix products  14.6 us (9%)
  waiting for transfers between devices  13.7 us (8%)
  other arithmetic  10.8 us (7%)
  between operations  2.92 us (2%)
    all_gather x1, blocking collectives, body(): gathered = lax.all_gather(packed_shard(basis), 'z', axis=0, tiled=True)  56.2 us
    all_to_all x1, blocking collectives, body(): lax.all_to_all(pieces, ('param', 'core'), 0, 0, tiled=True).sum(axis=0)  18.5 us
    ppermute x2, starting transfers between devices, swap_cores(): return lax.ppermute(array, 'core', [(0, 1), (1, 0)])  16.6 us
    all_to_all x1, waiting for transfers between devices, sent_to_all(): lax.all_to_all(jnp.broadcast_to(array[None], (peers, *array.shape)), axis...  13.7 us
    all_gather x1, blocking collectives, body(): everyone = lax.all_gather(column, 'core', axis=0, tiled=True)  7.34 us
    all_to_all x1, starting transfers between devices, sent_to_all(): lax.all_to_all(jnp.broadcast_to(array[None], (peers, *array.shape)), axis...  7.17 us
    dot_general x2, matrix products, contract(): lax.dot_general(rows, half_basis, (((1, 2), (0, 1)), ((), ())), preferred...  6.84 us
    dot_general x2, matrix products, lift(): lax.dot_general(phi_low, half_basis, (((1,), (2,)), ((), ())), preferred_...  6.78 us
  transfers between devices with their start and end apart: 3, of which 1 were waited for; matrix products, arithmetic and copies ran while one was open for 12% of the time, Pallas kernels for 0%

profile of v1, /device:TPU:1, one launch (start us, length us, event | category | flops | bytes accessed | tf_op | source)
XLA Modules:
  0.0 163.5 jit_solution(3833632551950099239)
XLA Ops:
  0.6 3.0 %pad_maximum_fusion = bf16[32,32768]{1,0:T(8,128)(2,1)} fusion(bf16[16,32768]{1,0:T(8,128)(2,1)} %param.4, bf16[16,32768]{1,0:T(8,128)(2,1)} %param.3), kind=kLoop, calls=%fused_computation.1 | loop fusion | flops 4194304 | bytes 4194304 | tf_op jit(solution)/shard_map/concatenate | solution.py:74
  3.7 3.3 %reshape.134 = bf16[32,16,2,1024]{3,2,1,0:T(2,128)(2,1)S(1)} reshape(bf16[32,32768]{1,0:T(8,128)(2,1)} %pad_maximum_fusion) | data formatting | bytes 4194304 | tf_op jit(solution)/shard_map/reshape | solution.py:74
  7.0 0.0 copy-start.2
  7.0 5.8 %constant_dynamic-slice_fusion.1 = (bf16[32,16,1,1024]{3,2,1,0:T(2,128)(2,1)}, bf16[32,16,1,1024]{3,2,1,0:T(2,128)(2,1)S(1)}) fusion(bf16[32,16,2,1024]{3,2,1,0:T(2,128)(2,1)S(1)} %reshape.134, s32[]{:T(128)S(6)} %select_n.47, s32[]{:T(128)S(6)} %select_n.48), kind=kLoop, calls=%fused_computation.51 | loop fusion | bytes 4194312 | tf_op jit(solution)/shard_map/jit(dynamic_index_in_dim)/dynamic_slice | solution.py:76
  12.7 1.1 copy.30
  13.9 8.8 %collective-permute-start = (bf16[32,16,1024]{2,0,1:T(8,128)(2,1)S(1)}, bf16[32,16,1024]{2,0,1:T(8,128)(2,1)}, u32[]{:S(2)}, u32[]{:S(2)}) collective-permute-start(bf16[32,16,1024]{2,0,1:T(8,128)(2,1)S(1)} %bitcast.44), channel_id=1, source_target_pairs={{0,1},{1,0},{2,3},{3,2},{4,5},{5,4},{6,7},{7,6},{8,9},{9,8},{10,11... | collective-permute-start | bytes 3145736 | tf_op jit(solution)/shard_map/ppermute | solution.py:15
  22.7 0.0 copy-done.2
  22.7 0.6 fusion.9
  24.1 0.1 fusion.10
  24.1 0.1 concatenate.49
  24.2 56.2 %all-gather.1 = f16[16640,128]{1,0:T(8,128)(2,1)S(1)} all-gather(f16[1040,128]{1,0:T(8,128)(2,1)S(1)} %concatenate.49), channel_id=1, replica_groups=mesh['param'=16,'z'=16,'core'=2] {'z'}, dimensions={0}, use_global_device_ids=true | all-gather | bytes 4526080 | tf_op jit(solution)/shard_map/all_gather | solution.py:78
  80.4 0.0 copy-start
  80.4 2.0 %copy-done = f16[16640,128]{1,0:T(8,128)(2,1)} copy-done((f16[16640,128]{1,0:T(8,128)(2,1)}, f16[16640,128]{1,0:T(8,128)(2,1)S(1)}, u32[]{:S(2)}) %copy-start) | copy-done | bytes 4259864
  82.3 0.1 copy.25
  82.4 0.0 copy-start.1
  82.4 5.4 %multiply_convert_fusion = bf16[16,1024,128]{2,1,0:T(8,128)(2,1)} fusion(f16[16,1040,128]{2,1,0:T(8,128)(2,1)} %bitcast.42, f32[16]{0:T(128)S(1)} %exponential_bitcast_fusion), kind=kLoop, calls=%fused_computation | loop fusion | flops 6291456 | bytes 8388672 | tf_op jit(solution)/shard_map/convert_element_type | solution.py:31
  87.9 7.8 %collective-permute-start.1 = (bf16[16,1024,128]{2,1,0:T(8,128)(2,1)}, bf16[16,1024,128]{2,1,0:T(8,128)(2,1)}, u32[]{:S(2)}, u32[]{:S(2)}) collective-permute-start(bf16[16,1024,128]{2,1,0:T(8,128)(2,1)} %multiply_convert_fusion), channel_id=1, source_target_pairs={{0,1},{1,0},{2,3},{3,2},{4,5},{5,4},{6,7},{7,6},{8,9},{9,8},{10,11... | collective-permute-start | bytes 12582920 | tf_op jit(solution)/shard_map/ppermute | solution.py:15
  95.7 0.0 copy-done.1
  95.7 3.6 %convolution_bitcast_fusion.1 = f32[32,128]{1,0:T(8,128)S(1)} fusion(bf16[16,1024,128]{2,1,0:T(8,128)(2,1)} %multiply_convert_fusion, bf16[32,16,1,1024]{3,2,1,0:T(2,128)(2,1)S(1)} %copy-done.1), kind=kOutput, calls=%fused_computation.12 | convolution fusion | flops 134217728 | bytes 5259264 | tf_op jit(solution)/shard_map/dot_general | solution.py:57
  99.3 0.0 collective-permute-done
  99.3 3.3 %convolution_bitcast_fusion = f32[32,128]{1,0:T(8,128)S(1)} fusion(bf16[32,16,1024]{2,0,1:T(8,128)(2,1)} %collective-permute-done, bf16[16,1024,128]{2,1,0:T(8,128)(2,1)} %multiply_convert_fusion), kind=kOutput, calls=%fused_computation.11 | convolution fusion | flops 134217728 | bytes 5259264 | tf_op jit(solution)/shard_map/dot_general | solution.py:57
  102.6 0.1 broadcast_in_dim.4
  102.7 18.5 %all_to_all.10 = f32[32,16,256]{2,1,0:T(8,128)S(1)} all-to-all(f32[32,16,256]{2,1,0:T(8,128)S(1)} %bitcast.43), channel_id=1, replica_groups=mesh['param'=16,'z'=16,'core'=2] {'param','core'}, dimensions={0} | all-to-all | bytes 1048576 | tf_op jit(solution)/shard_map/all_to_all | solution.py:90
  121.3 0.7 broadcast_in_dim.5
  122.0 7.2 %all-to-all-start.1 = ((f32[16,16,256]{2,1,0:T(8,128)}), f32[16,16,256]{2,1,0:T(8,128)S(1)}, u32[]{:S(2)}, u32[]{:S(2)}) async-start(f32[16,16,256]{2,1,0:T(8,128)} %broadcast_in_dim.5), calls=%async_computation.1 | async-start | bytes 524288 | tf_op jit(solution)/shard_map/all_to_all | solution.py:51
  129.2 0.1 multiply_reduce_fusion.2
  129.3 13.7 %all-to-all-done.1 = f32[16,16,256]{2,1,0:T(8,128)S(1)} async-done(((f32[16,16,256]{2,1,0:T(8,128)}), f32[16,16,256]{2,1,0:T(8,128)S(1)}, u32[]{:S(2)}, u32[]{:S(2)}) %all-to-all-start.1) | async-done | bytes 262176 | tf_op jit(solution)/shard_map/all_to_all | solution.py:51
  143.0 7.3 %all_gather.7 = f32[512,256]{1,0:T(8,128)S(1)} all-gather(f32[256,256]{1,0:T(8,128)S(1)} %bitcast.45), channel_id=1, replica_groups=mesh['param'=16,'z'=16,'core'=2] {'core'}, dimensions={0}, use_global_device_ids=true | all-gather | bytes 786432 | tf_op jit(solution)/shard_map/all_gather | solution.py:92
  150.3 0.7 multiply_reduce_fusion.1
  151.7 0.6 multiply_reduce_fusion.3
  152.9 0.4 fusion.22
  153.4 0.2 fusion.11
  153.6 0.3 fusion.8
  153.9 0.0 copy-start.3
  153.9 3.4 %fusion = bf16[16,16,1024]{2,0,1:T(8,128)(2,1)S(1)} fusion(bf16[16,1024,128]{2,1,0:T(8,128)(2,1)} %multiply_convert_fusion, f32[16,128]{1,0:T(8,128)S(1)} %fusion.8), kind=kOutput, calls=%fused_computation.4 | convolution fusion | flops 67635200 | bytes 4726784 | tf_op jit(solution)/shard_map/dot_general | solution.py:63
  157.3 0.0 collective-permute-done.1
  157.3 3.4 %select_bitcast_fusion.1 = (bf16[16,16,1,1024]{3,0,1,2:T(8,128)(2,1)S(1)}, bf16[16,16,1,1024]{3,0,1,2:T(8,128)(2,1)S(1)}) fusion(bf16[16,16,1024]{2,0,1:T(8,128)(2,1)S(1)} %fusion, pred[]{:T(512)S(6)} %eq.2, bf16[16,1024,128]{2,1,0:T(8,128)(2,1)} %collective-permute-done.1, f32[16,128]{1,0:T(8,128)S(1)} %fusion.8), kind=kOutput, calls=%fused_computation.25 | convolution fusion | flops 68159488 | bytes 5775361 | tf_op jit(solution)/shard_map/dot_general | solution.py:63
  160.7 0.0 copy-done.3
  160.7 0.1 pad_maximum_fusion.1
  160.8 1.1 copy.23
  161.9 1.6 reshape.138
  (7 shorter events, 0.1 us)
Async XLA Ops:
  7.0 15.7 %copy-start.2 = (bf16[1024,128]{1,0:T(8,128)(2,1)S(1)}, bf16[1024,128]{1,0:T(8,128)(2,1)}, u32[]{:S(2)}) copy-start(bf16[1024,128]{1,0:T(8,128)(2,1)} %param.5) | copy-start | bytes 786436
  13.9 85.4 %collective-permute-start = (bf16[32,16,1024]{2,0,1:T(8,128)(2,1)S(1)}, bf16[32,16,1024]{2,0,1:T(8,128)(2,1)}, u32[]{:S(2)}, u32[]{:S(2)}) collective-permute-start(bf16[32,16,1024]{2,0,1:T(8,128)(2,1)S(1)} %bitcast.44), channel_id=1, source_target_pairs={{0,1},{1,0},{2,3},{3,2},{4,5},{5,4},{6,7},{7,6},{8,9},{9,8},{10,11... | collective-permute-start | bytes 3145736 | tf_op jit(solution)/shard_map/ppermute | solution.py:15
  80.4 2.0 %copy-start = (f16[16640,128]{1,0:T(8,128)(2,1)}, f16[16640,128]{1,0:T(8,128)(2,1)S(1)}, u32[]{:S(2)}) copy-start(f16[16640,128]{1,0:T(8,128)(2,1)S(1)} %all-gather.1) | copy-start | bytes 12779524
  82.4 13.2 %copy-start.1 = (bf16[32,16,1,1024]{3,2,1,0:T(2,128)(2,1)S(1)}, bf16[32,16,1,1024]{3,2,1,0:T(2,128)(2,1)}, u32[]{:S(2)}) copy-start(bf16[32,16,1,1024]{3,2,1,0:T(2,128)(2,1)} %get-tuple-element.5) | copy-start | bytes 3145732
  87.9 69.4 %collective-permute-start.1 = (bf16[16,1024,128]{2,1,0:T(8,128)(2,1)}, bf16[16,1024,128]{2,1,0:T(8,128)(2,1)}, u32[]{:S(2)}, u32[]{:S(2)}) collective-permute-start(bf16[16,1024,128]{2,1,0:T(8,128)(2,1)} %multiply_convert_fusion), channel_id=1, source_target_pairs={{0,1},{1,0},{2,3},{3,2},{4,5},{5,4},{6,7},{7,6},{8,9},{9,8},{10,11... | collective-permute-start | bytes 12582920 | tf_op jit(solution)/shard_map/ppermute | solution.py:15
  122.0 21.0 %all-to-all-start.1 = ((f32[16,16,256]{2,1,0:T(8,128)}), f32[16,16,256]{2,1,0:T(8,128)S(1)}, u32[]{:S(2)}, u32[]{:S(2)}) async-start(f32[16,16,256]{2,1,0:T(8,128)} %broadcast_in_dim.5), calls=%async_computation.1 | async-start | bytes 524288 | tf_op jit(solution)/shard_map/all_to_all | solution.py:51
  153.9 6.8 %copy-start.3 = (f32[16,128]{1,0:T(8,128)}, f32[16,128]{1,0:T(8,128)S(1)}, u32[]{:S(2)}) copy-start(f32[16,128]{1,0:T(8,128)S(1)} %fusion.8) | copy-start | bytes 24580

commit v2 on v1

v2 whole, which is shorter than its diff:
```python
import math

import jax
import jax.numpy as jnp
from jax import lax
from jax.experimental import pallas as pl
from jax.experimental.pallas import tpu as pltpu
from jax.sharding import Mesh, PartitionSpec as P

P_SIZE = 524288
R = 128
TAIL = 16
TOP = 15.0
HIGHEST = lax.Precision.HIGHEST
ACROSS = (((1,), (1,)), ((), ()))
CHUNKS = 4
VMEM = pl.BlockSpec(memory_space=pltpu.VMEM)
ANY = pl.BlockSpec(memory_space=pl.ANY)
SMEM = pl.BlockSpec(memory_space=pltpu.SMEM)


def swap_cores(array):
    return lax.ppermute(array, "core", [(0, 1), (1, 0)])


def packed_shard(basis):
    wide = basis.astype(jnp.float32)
    largest = jnp.maximum(jnp.max(jnp.abs(wide)), 1e-30)
    power = jnp.ceil(jnp.log2(largest))
    scaled = (wide * jnp.exp2(TOP - power)).astype(jnp.float16)
    tail = jnp.full((TAIL, basis.shape[1]), power, jnp.float32).astype(jnp.float16)
    return jnp.concatenate([scaled, tail], axis=0)


def unpacked(gathered, shards):
    rows = gathered.reshape(shards, -1, gathered.shape[1])
    power = rows[:, -TAIL:, :].astype(jnp.float32)[:, :1, :1]
    wide = rows[:, :-TAIL, :].astype(jnp.float32) * jnp.exp2(power - TOP)
    return wide.astype(jnp.bfloat16)


def chunk_copies(source_ref, target_ref, sems):
    size = source_ref.shape[0] // CHUNKS
    return [
        pltpu.make_async_copy(
            source_ref.at[pl.ds(k * size, size)], target_ref.at[pl.ds(k * size, size)], sems.at[k]
        )
        for k in range(CHUNKS)
    ]


def contract_kernel(core_ref, p_ref, s_ref, other_p_ref, other_s_ref, half_hbm, out_ref, half_ref, sems):
    core = core_ref[0]
    shards, depth, cols = half_ref.shape
    rows = p_ref.shape[0]
    copies = chunk_copies(half_hbm, half_ref, sems)
    for copy in copies:
        copy.start()
    total = jnp.zeros((4 * rows, cols), jnp.float32)
    for i in range(shards):
        if i % (shards // CHUNKS) == 0:
            copies[i // (shards // CHUNKS)].wait()
        at = pl.ds(pl.multiple_of((2 * i + core) * depth, depth), depth)
        block = jnp.concatenate([r[:, at] for r in (p_ref, s_ref, other_p_ref, other_s_ref)], axis=0)
        total += jnp.dot(block, half_ref[i], preferred_element_type=jnp.float32)
    own = jnp.concatenate([total[:rows], total[rows : 2 * rows]], axis=1)
    other = jnp.concatenate([total[2 * rows : 3 * rows], total[3 * rows :]], axis=1)
    out_ref[core] = own
    out_ref[1 - core] = other


def contract(core, particles, scores, other_p, other_s, half):
    rows, cols = particles.shape[0], half.shape[2]
    return pl.pallas_call(
        contract_kernel,
        out_shape=jax.ShapeDtypeStruct((2, rows, 2 * cols), jnp.float32),
        in_specs=[SMEM] + [VMEM] * 4 + [ANY],
        out_specs=VMEM,
        scratch_shapes=[pltpu.VMEM(half.shape, half.dtype), pltpu.SemaphoreType.DMA((CHUNKS,))],
        compiler_params=pltpu.CompilerParams(vmem_limit_bytes=24 << 20),
        cost_estimate=pl.CostEstimate(
            flops=2 * 4 * rows * half.size, bytes_accessed=2 * half.size, transcendentals=0
        ),
    )(core, particles, scores, other_p, other_s, half)


def stein_terms(own, both):
    count, cols = both.shape[0], own.shape[1]
    every = both[:, :cols]
    squares = every * every
    center = jnp.sum(every, axis=0, keepdims=True) / count
    mean_sq = jnp.sum(squares) / count
    width = 2.0 * (mean_sq - jnp.sum(center * center)) / math.log(count) + 1e-06
    every_sq = lax.dot_general(
        jnp.ones_like(own), squares, ACROSS, precision=HIGHEST, preferred_element_type=jnp.float32
    )
    cross = lax.dot_general(
        own, every, ACROSS, precision=HIGHEST, preferred_element_type=jnp.float32
    )
    dist = jnp.sum(own * own, axis=1, keepdims=True) + every_sq - 2.0 * cross
    kern = jnp.exp(-dist / width)
    pulled = jnp.dot(kern, both, precision=HIGHEST, preferred_element_type=jnp.float32)
    total = jnp.sum(kern, axis=1, keepdims=True)
    return (pulled[:, cols:] + (2.0 / width) * (own * total - pulled[:, :cols])) / count


def finish_kernel(
    core_ref, own_ref, every_ref, half_hbm, other_hbm, velocity_hbm, phi_ref,
    half_ref, other_ref, velocity_ref, half_sems, other_sems, out_sems,
):
    core = core_ref[0]
    shards, depth, cols = half_ref.shape
    copies = tuple(
        zip(
            chunk_copies(half_hbm, half_ref, half_sems),
            chunk_copies(other_hbm, other_ref, other_sems),
        )
    )
    for pair in copies:
        for copy in pair:
            copy.start()
    phi = stein_terms(own_ref[:, :cols], every_ref[...])
    phi_ref[...] = phi
    low = phi.astype(jnp.bfloat16)
    scale = math.sqrt(P_SIZE / R)
    each = shards // CHUNKS
    span = 2 * each * depth
    outs = []
    for k in range(CHUNKS):
        for copy in copies[k]:
            copy.wait()
        for i in range(k * each, (k + 1) * each):
            for ref, place in ((half_ref, core), (other_ref, 1 - core)):
                lifted = lax.dot_general(low, ref[i], ACROSS, preferred_element_type=jnp.float32)
                at = pl.ds(pl.multiple_of((2 * i + place) * depth, depth), depth)
                velocity_ref[:, at] = (lifted * scale).astype(jnp.bfloat16)
        part = pl.ds(k * span, span)
        out = pltpu.make_async_copy(velocity_ref.at[:, part], velocity_hbm.at[:, part], out_sems.at[k])
        out.start()
        outs.append(out)
    for out in outs:
        out.wait()


def finish(core, own, everyone, half, other_half):
    rows, cols = own.shape[0], half.shape[2]
    dims = 2 * half.shape[0] * half.shape[1]
    sems = pltpu.SemaphoreType.DMA((CHUNKS,))
    return pl.pallas_call(
        finish_kernel,
        out_shape=(
            jax.ShapeDtypeStruct((rows, dims), jnp.bfloat16),
            jax.ShapeDtypeStruct((rows, cols), jnp.float32),
        ),
        in_specs=[SMEM, VMEM, VMEM, ANY, ANY],
        out_specs=(ANY, VMEM),
        scratch_shapes=[
            pltpu.VMEM(half.shape, half.dtype),
            pltpu.VMEM(half.shape, half.dtype),
            pltpu.VMEM((rows, dims), jnp.bfloat16),
            sems,
            sems,
            sems,
        ],
        compiler_params=pltpu.CompilerParams(vmem_limit_bytes=24 << 20),
        cost_estimate=pl.CostEstimate(
            flops=4 * rows * half.size, bytes_accessed=4 * half.size, transcendentals=0
        ),
    )(core, own, everyone, half, other_half)


def sent_to_all(array, axis):
    peers = lax.axis_size(axis)
    return lax.all_to_all(
        jnp.broadcast_to(array[None], (peers, *array.shape)), axis, 0, 0, tiled=True
    )


def body(particles, scores, basis):
    rows = particles.shape[0]
    shards = lax.axis_size("z")
    peers = lax.axis_size("param")
    core = lax.axis_index("core").astype(jnp.int32)[None]
    other_p = swap_cores(particles)
    other_s = swap_cores(scores)
    packed, other_p, other_s = lax.optimization_barrier((packed_shard(basis), other_p, other_s))
    gathered = lax.all_gather(packed, "z", axis=0, tiled=True)
    half = unpacked(gathered, shards)
    other_half = swap_cores(half)
    pair = contract(core, particles, scores, other_p, other_s, half)
    pieces = jnp.broadcast_to(pair[None], (peers, *pair.shape)).reshape(2 * peers, rows, -1)
    summed = lax.all_to_all(pieces, ("param", "core"), 0, 0, tiled=True).sum(axis=0)
    column = sent_to_all(summed, "z").reshape(shards * rows, -1)
    everyone = lax.all_gather(column, "core", axis=0, tiled=True)
    velocity, phi = finish(core, summed, everyone, half, other_half)
    return (velocity, phi)


def solution(mesh):
    inner = Mesh(mesh.devices.reshape(mesh.devices.shape[0], -1, 2), ("param", "z", "core"))
    dom = ("z", "core")
    in_specs = (P(dom, "param"), P(dom, "param"), P(("param", "z", "core"), None))
    out_specs = (P(dom, "param"), P(dom, None))
    return jax.shard_map(body, mesh=inner, in_specs=in_specs, out_specs=out_specs, check_vma=False)
```

time: 164 us -> 141 us (0.86)
  blocking collectives: 82 us -> 103 us
  matrix products: 14.6 us -> 0 us
  waiting for transfers between devices: 13.7 us -> 0.01 us
  local copies, waits for them, and re-layouts: 15.8 us -> 2.32 us
  Pallas kernels: 0 us -> 8.9 us
  other arithmetic: 10.8 us -> 5.93 us
  starting transfers between devices: 23.7 us -> 19.1 us
    all_to_all x0 -> x1, blocking collectives: none -> 20.8 us  [sent_to_all(): lax.all_to_all(jnp.broadcast_to(array[None], (peers, *array.shape)), axis...]
    dot_general x7 -> x0, matrix products: 14.6 us -> none  [the longest x2 6.84 us: contract(): lax.dot_general(rows, half_basis, (((1, 2), (0, 1)), ((), ())), preferred...]
    all_to_all x1 -> x0, waiting for transfers between devices: 13.7 us -> none  [sent_to_all(): lax.all_to_all(jnp.broadcast_to(array[None], (peers, *array.shape)), axis...]
    pallas_call x0 -> x2, Pallas kernels: none -> 8.9 us  [the longest x1 6.38 us: finish(): pl.pallas_call(finish_kernel, out_shape=(jax.ShapeDtypeStruct((rows, dims...]
    all_to_all x1 -> x0, starting transfers between devices: 7.17 us -> none  [sent_to_all(): lax.all_to_all(jnp.broadcast_to(array[None], (peers, *array.shape)), axis...]
    dynamic_slice x1 -> x0, local copies, waits for them, and re-layouts: 5.76 us -> none  [body(): mine = lax.dynamic_index_in_dim(both, core, 2, keepdims=False)]
    reshape x2 -> x0, local copies, waits for them, and re-layouts: 4.91 us -> none  [the longest x1 3.3 us: body(): jnp.concatenate([particles, scores], axis=0)]
    concatenate x1 -> x0, other arithmetic: 3.03 us -> none  [body(): jnp.concatenate([particles, scores], axis=0)]
  transfers between devices with their start and end apart: 3 -> 3, of which waited for: 1 -> 0; matrix products, arithmetic and copies ran while one was open for 12% -> 2% of each run, Pallas kernels for 0% -> 2%
where the time goes in v2:
time: 141 us
  blocking collectives  103 us (73%)
  starting transfers between devices  19.1 us (14%)
  Pallas kernels  8.9 us (6%)
  other arithmetic  5.93 us (4%)
  local copies, waits for them, and re-layouts  2.32 us (2%)
  between operations  1.49 us (1%)
    all_gather x1, blocking collectives, body(): gathered = lax.all_gather(packed, 'z', axis=0, tiled=True)  56.3 us
    all_to_all x1, blocking collectives, sent_to_all(): lax.all_to_all(jnp.broadcast_to(array[None], (peers, *array.shape)), axis...  20.8 us
    ppermute x3, starting transfers between devices, swap_cores(): return lax.ppermute(array, 'core', [(0, 1), (1, 0)])  19.1 us
    all_to_all x1, blocking collectives, body(): lax.all_to_all(pieces, ('param', 'core'), 0, 0, tiled=True).sum(axis=0)  18.5 us
    all_gather x1, blocking collectives, body(): everyone = lax.all_gather(column, 'core', axis=0, tiled=True)  7.16 us
    pallas_call x1, Pallas kernels, finish(): pl.pallas_call(finish_kernel, out_shape=(jax.ShapeDtypeStruct((rows, dims...  6.38 us
    convert_element_type x1, other arithmetic, unpacked(): return wide.astype(jnp.bfloat16)  3.06 us
  transfers between devices with their start and end apart: 3, of which 0 were waited for; matrix products, arithmetic and copies ran while one was open for 2% of the time, Pallas kernels for 2%

profile of v2, /device:TPU:1, one launch (start us, length us, event | category | flops | bytes accessed | tf_op | source)
XLA Modules:
  0.0 140.5 jit_solution(5239994096646493235)
XLA Ops:
  0.6 8.8 %collective-permute-start = (bf16[16,32768]{1,0:T(8,128)(2,1)}, bf16[16,32768]{1,0:T(8,128)(2,1)S(1)}, u32[]{:S(2)}, u32[]{:S(2)}) collective-permute-start(bf16[16,32768]{1,0:T(8,128)(2,1)} %p_ref.1), channel_id=1, source_target_pairs={{0,1},{1,0},{2,3},{3,2},{4,5},{5,4},{6,7},{7,6},{8,9},{9,8},{10,11... | collective-permute-start | bytes 3145736 | tf_op jit(solution)/shard_map/ppermute | solution.py:23
  9.4 1.9 %collective-permute-start.1 = (bf16[16,32768]{1,0:T(8,128)(2,1)}, bf16[16,32768]{1,0:T(8,128)(2,1)S(1)}, u32[]{:S(2)}, u32[]{:S(2)}) collective-permute-start(bf16[16,32768]{1,0:T(8,128)(2,1)} %s_ref.1), channel_id=1, source_target_pairs={{0,1},{1,0},{2,3},{3,2},{4,5},{5,4},{6,7},{7,6},{8,9},{9,8},{10,11... | collective-permute-start | bytes 3145736 | tf_op jit(solution)/shard_map/ppermute | solution.py:23
  11.4 1.6 %fusion = f32[]{:T(128)} fusion(bf16[1024,128]{1,0:T(8,128)(2,1)} %param.5), kind=kLoop, calls=%fused_computation.3 | loop fusion | flops 393215 | bytes 262148 | tf_op jit(solution)/shard_map/reduce_max | solution.py:28
  13.7 1.0 fusion.1
  14.7 0.1 concatenate.3
  14.8 0.0 collective-permute-done.other_p_ref
  14.8 0.0 collective-permute-done.1.other_s_ref
  14.8 0.0 copy-start.2
  14.8 1.0 copy-done.2
  15.8 56.3 %all-gather.1 = f16[16640,128]{1,0:T(8,128)(2,1)S(1)} all-gather(f16[1040,128]{1,0:T(8,128)(2,1)S(1)} %concatenate.3), channel_id=1, replica_groups=mesh['param'=16,'z'=16,'core'=2] {'z'}, dimensions={0}, use_global_device_ids=true | all-gather | bytes 4526080 | tf_op jit(solution)/shard_map/all_gather | solution.py:187
  72.1 0.0 copy-start
  72.1 0.0 copy-start.1
  72.1 0.2 fusion.5
  72.3 3.1 %multiply_convert_fusion.half_hbm = bf16[16,1024,128]{2,1,0:T(8,128)(2,1)} fusion(f16[16,1040,128]{2,1,0:T(8,128)(2,1)S(1)} %bitcast.5, f32[16]{0:T(128)S(1)} %fusion.5), kind=kLoop, calls=%fused_computation | loop fusion | flops 6291456 | bytes 8388672 | tf_op jit(solution)/shard_map/convert_element_type | solution.py:39
  75.4 8.4 %collective-permute-start.2 = (bf16[16,1024,128]{2,1,0:T(8,128)(2,1)}, bf16[16,1024,128]{2,1,0:T(8,128)(2,1)}, u32[]{:S(2)}, u32[]{:S(2)}) collective-permute-start(bf16[16,1024,128]{2,1,0:T(8,128)(2,1)} %multiply_convert_fusion.half_hbm), channel_id=1, source_target_pairs={{0,1},{1,0},{2,3},{3,2},{4,5},{5,4},{6,7},{7,6},{8,9},{9,8},{10,11... | collective-permute-start | bytes 12582920 | tf_op jit(solution)/shard_map/ppermute | solution.py:23
  83.7 0.0 copy-done
  83.7 0.0 copy-done.1
  83.8 0.0 copy-start.3
  83.8 1.2 copy-done.3
  85.0 2.5 %shard_map.50 = f32[2,16,256]{2,1,0:T(8,128)S(1)} custom-call(s32[1]{0:T(128)} %bitcast.core_ref, bf16[16,32768]{1,0:T(8,128)(2,1)S(1)} %copy-done, bf16[16,32768]{1,0:T(8,128)(2,1)S(1)} %copy-done.1, bf16[16,32768]{1,0:T(8,128)(2,1)S(1)} %collective-permute-done.other_p_ref, bf16[16,32768]{1,0:T(8,128)(2,1)S(1)} %copy-done.3, ...), custom_call_target="tpu_custom_call" | custom-call | flops 268435456 | bytes 4194304 | tf_op jit(solution)/shard_map/pallas_call | solution.py:74
  87.5 0.1 broadcast_in_dim.7
  87.6 18.5 %all_to_all.10 = f32[32,16,256]{2,1,0:T(8,128)S(1)} all-to-all(f32[32,16,256]{2,1,0:T(8,128)S(1)} %bitcast.6), channel_id=1, replica_groups=mesh['param'=16,'z'=16,'core'=2] {'param','core'}, dimensions={0} | all-to-all | bytes 1048576 | tf_op jit(solution)/shard_map/all_to_all | solution.py:192
  106.2 20.8 %all_to_all.11 = f32[16,16,256]{2,1,0:T(8,128)S(1)} all-to-all(f32[16,16,256]{2,1,0:T(8,128)S(1)} %broadcast_in_dim.8), channel_id=1, replica_groups=mesh['param'=16,'z'=16,'core'=2] {'z'}, dimensions={0} | all-to-all | bytes 524288 | tf_op jit(solution)/shard_map/all_to_all | solution.py:174
  127.0 7.2 %all_gather.7.every_ref = f32[512,256]{1,0:T(8,128)S(1)} all-gather(f32[256,256]{1,0:T(8,128)S(1)} %bitcast.7), channel_id=1, replica_groups=mesh['param'=16,'z'=16,'core'=2] {'core'}, dimensions={0}, use_global_device_ids=true | all-gather | bytes 786432 | tf_op jit(solution)/shard_map/all_gather | solution.py:194
  134.1 0.0 collective-permute-done.2.other_hbm
  134.1 6.4 %shard_map.51 = (bf16[16,32768]{1,0:T(8,128)(2,1)}, f32[16,128]{1,0:T(8,128)}) custom-call(s32[1]{0:T(128)} %bitcast.core_ref, f32[16,256]{1,0:T(8,128)S(1)} %reduce_sum.9.own_ref, f32[512,256]{1,0:T(8,128)S(1)} %all_gather.7.every_ref, bf16[16,1024,128]{2,1,0:T(8,128)(2,1)} %multiply_convert_fusion.half_hbm, ...), custom_call_target="tpu_custom_call" | custom-call | flops 134217728 | bytes 8388608 | tf_op jit(solution)/shard_map/pallas_call | solution.py:149
  (2 shorter events, 0.1 us)
Async XLA Ops:
  0.6 14.2 %collective-permute-start = (bf16[16,32768]{1,0:T(8,128)(2,1)}, bf16[16,32768]{1,0:T(8,128)(2,1)S(1)}, u32[]{:S(2)}, u32[]{:S(2)}) collective-permute-start(bf16[16,32768]{1,0:T(8,128)(2,1)} %p_ref.1), channel_id=1, source_target_pairs={{0,1},{1,0},{2,3},{3,2},{4,5},{5,4},{6,7},{7,6},{8,9},{9,8},{10,11... | collective-permute-start | bytes 3145736 | tf_op jit(solution)/shard_map/ppermute | solution.py:23
  9.4 5.4 %collective-permute-start.1 = (bf16[16,32768]{1,0:T(8,128)(2,1)}, bf16[16,32768]{1,0:T(8,128)(2,1)S(1)}, u32[]{:S(2)}, u32[]{:S(2)}) collective-permute-start(bf16[16,32768]{1,0:T(8,128)(2,1)} %s_ref.1), channel_id=1, source_target_pairs={{0,1},{1,0},{2,3},{3,2},{4,5},{5,4},{6,7},{7,6},{8,9},{9,8},{10,11... | collective-permute-start | bytes 3145736 | tf_op jit(solution)/shard_map/ppermute | solution.py:23
  14.8 1.0 copy-start.2
  72.1 11.6 %copy-start = (bf16[16,32768]{1,0:T(8,128)(2,1)S(1)}, bf16[16,32768]{1,0:T(8,128)(2,1)}, u32[]{:S(2)}) copy-start(bf16[16,32768]{1,0:T(8,128)(2,1)} %p_ref.1) | copy-start | bytes 3145732
  72.1 11.7 %copy-start.1 = (bf16[16,32768]{1,0:T(8,128)(2,1)S(1)}, bf16[16,32768]{1,0:T(8,128)(2,1)}, u32[]{:S(2)}) copy-start(bf16[16,32768]{1,0:T(8,128)(2,1)} %s_ref.1) | copy-start | bytes 3145732
  75.4 58.8 %collective-permute-start.2 = (bf16[16,1024,128]{2,1,0:T(8,128)(2,1)}, bf16[16,1024,128]{2,1,0:T(8,128)(2,1)}, u32[]{:S(2)}, u32[]{:S(2)}) collective-permute-start(bf16[16,1024,128]{2,1,0:T(8,128)(2,1)} %multiply_convert_fusion.half_hbm), channel_id=1, source_target_pairs={{0,1},{1,0},{2,3},{3,2},{4,5},{5,4},{6,7},{7,6},{8,9},{9,8},{10,11... | collective-permute-start | bytes 12582920 | tf_op jit(solution)/shard_map/ppermute | solution.py:23
  83.8 1.2 copy-start.3

commit v3 on v2

--- a/solution.py
+++ b/solution.py
@@ -14,8 +14,9 @@
 HIGHEST = lax.Precision.HIGHEST
 ACROSS = (((1,), (1,)), ((), ()))
 CHUNKS = 4
+PIECES = 8
 VMEM = pl.BlockSpec(memory_space=pltpu.VMEM)
-ANY = pl.BlockSpec(memory_space=pl.ANY)
+HBM = pl.BlockSpec(memory_space=pltpu.HBM)
 SMEM = pl.BlockSpec(memory_space=pltpu.SMEM)
 
 
@@ -23,13 +24,52 @@
     return lax.ppermute(array, "core", [(0, 1), (1, 0)])
 
 
-def packed_shard(basis):
-    wide = basis.astype(jnp.float32)
-    largest = jnp.maximum(jnp.max(jnp.abs(wide)), 1e-30)
-    power = jnp.ceil(jnp.log2(largest))
-    scaled = (wide * jnp.exp2(TOP - power)).astype(jnp.float16)
-    tail = jnp.full((TAIL, basis.shape[1]), power, jnp.float32).astype(jnp.float16)
-    return jnp.concatenate([scaled, tail], axis=0)
+def prepare_kernel(
+    core_ref, p_hbm, s_hbm, basis_hbm, theirs_ref, packed_ref, basis_ref, sems, basis_sem
+):
+    core = core_ref[0]
+    rows = p_hbm.shape[0]
+    depth = basis_ref.shape[0]
+    fetch = pltpu.make_async_copy(basis_hbm, basis_ref, basis_sem)
+    fetch.start()
+    copies = []
+    for k, source in enumerate((p_hbm, s_hbm)):
+        for i in range(theirs_ref.shape[1] // depth):
+            at = pl.ds(pl.multiple_of((2 * i + 1 - core) * depth, depth), depth)
+            target = theirs_ref.at[pl.ds(k * rows, rows), pl.ds(i * depth, depth)]
+            copies.append(pltpu.make_async_copy(source.at[:, at], target, sems.at[k, i]))
+    for copy in copies:
+        copy.start()
+    fetch.wait()
+    wide = basis_ref[...].astype(jnp.float32)
+    largest = jnp.max(jnp.max(jnp.abs(wide), axis=0, keepdims=True), axis=1, keepdims=True)
+    power = jnp.ceil(jnp.log2(jnp.maximum(largest, 1e-30)))
+    packed_ref[:depth] = (wide * jnp.exp2(TOP - power)).astype(jnp.bfloat16)
+    packed_ref[depth:] = jnp.broadcast_to(power, (TAIL, wide.shape[1])).astype(jnp.bfloat16)
+    for copy in copies:
+        copy.wait()
+
+
+def prepare(core, particles, scores, basis):
+    rows, cols = particles.shape
+    depth = basis.shape[0]
+    return pl.pallas_call(
+        prepare_kernel,
+        out_shape=(
+            jax.ShapeDtypeStruct((2 * rows, cols // 2), particles.dtype),
+            jax.ShapeDtypeStruct((depth + TAIL, basis.shape[1]), jnp.bfloat16),
+        ),
+        in_specs=[SMEM, HBM, HBM, HBM],
+        out_specs=(VMEM, VMEM),
+        scratch_shapes=[
+            pltpu.VMEM(basis.shape, basis.dtype),
+            pltpu.SemaphoreType.DMA((2, cols // 2 // depth)),
+            pltpu.SemaphoreType.DMA,
+        ],
+        cost_estimate=pl.CostEstimate(
+            flops=2 * basis.size, bytes_accessed=4 * particles.size, transcendentals=0
+        ),
+    )(core, particles, scores, basis)
 
 
 def unpacked(gathered, shards):
@@ -40,16 +80,17 @@
 
 
 def chunk_copies(source_ref, target_ref, sems):
-    size = source_ref.shape[0] // CHUNKS
+    chunks = sems.shape[0]
+    size = source_ref.shape[0] // chunks
     return [
         pltpu.make_async_copy(
             source_ref.at[pl.ds(k * size, size)], target_ref.at[pl.ds(k * size, size)], sems.at[k]
         )
-        for k in range(CHUNKS)
+        for k in range(chunks)
     ]
 
 
-def contract_kernel(core_ref, p_ref, s_ref, other_p_ref, other_s_ref, half_hbm, out_ref, half_ref, sems):
+def contract_kernel(core_ref, p_ref, s_ref, others_ref, half_hbm, out_ref, half_ref, sems):
     core = core_ref[0]
     shards, depth, cols = half_ref.shape
     rows = p_ref.shape[0]
@@ -61,7 +102,8 @@
         if i % (shards // CHUNKS) == 0:
             copies[i // (shards // CHUNKS)].wait()
         at = pl.ds(pl.multiple_of((2 * i + core) * depth, depth), depth)
-        block = jnp.concatenate([r[:, at] for r in (p_ref, s_ref, other_p_ref, other_s_ref)], axis=0)
+        theirs = others_ref[:, i * depth : (i + 1) * depth]
+        block = jnp.concatenate([p_ref[:, at], s_ref[:, at], theirs], axis=0)
         total += jnp.dot(block, half_ref[i], preferred_element_type=jnp.float32)
     own = jnp.concatenate([total[:rows], total[rows : 2 * rows]], axis=1)
     other = jnp.concatenate([total[2 * rows : 3 * rows], total[3 * rows :]], axis=1)
@@ -69,31 +111,29 @@
     out_ref[1 - core] = other
 
 
-def contract(core, particles, scores, other_p, other_s, half):
+def contract(core, particles, scores, others, half):
     rows, cols = particles.shape[0], half.shape[2]
     return pl.pallas_call(
         contract_kernel,
         out_shape=jax.ShapeDtypeStruct((2, rows, 2 * cols), jnp.float32),
-        in_specs=[SMEM] + [VMEM] * 4 + [ANY],
+        in_specs=[SMEM] + [VMEM] * 3 + [HBM],
         out_specs=VMEM,
         scratch_shapes=[pltpu.VMEM(half.shape, half.dtype), pltpu.SemaphoreType.DMA((CHUNKS,))],
         compiler_params=pltpu.CompilerParams(vmem_limit_bytes=24 << 20),
         cost_estimate=pl.CostEstimate(
             flops=2 * 4 * rows * half.size, bytes_accessed=2 * half.size, transcendentals=0
         ),
-    )(core, particles, scores, other_p, other_s, half)
+    )(core, particles, scores, others, half)
 
 
 def stein_terms(own, both):
     count, cols = both.shape[0], own.shape[1]
     every = both[:, :cols]
-    squares = every * every
+    squares = jnp.sum(every * every, axis=1, keepdims=True)
     center = jnp.sum(every, axis=0, keepdims=True) / count
     mean_sq = jnp.sum(squares) / count
     width = 2.0 * (mean_sq - jnp.sum(center * center)) / math.log(count) + 1e-06
-    every_sq = lax.dot_general(
-        jnp.ones_like(own), squares, ACROSS, precision=HIGHEST, preferred_element_type=jnp.float32
-    )
+    every_sq = jnp.broadcast_to(squares, (count, cols)).T[: own.shape[0]]
     cross = lax.dot_general(
         own, every, ACROSS, precision=HIGHEST, preferred_element_type=jnp.float32
     )
@@ -123,10 +163,10 @@
     phi_ref[...] = phi
     low = phi.astype(jnp.bfloat16)
     scale = math.sqrt(P_SIZE / R)
-    each = shards // CHUNKS
+    each = shards // PIECES
     span = 2 * each * depth
     outs = []
-    for k in range(CHUNKS):
+    for k in range(PIECES):
         for copy in copies[k]:
             copy.wait()
         for i in range(k * each, (k + 1) * each):
@@ -145,15 +185,15 @@
 def finish(core, own, everyone, half, other_half):
     rows, cols = own.shape[0], half.shape[2]
     dims = 2 * half.shape[0] * half.shape[1]
-    sems = pltpu.SemaphoreType.DMA((CHUNKS,))
+    sems = pltpu.SemaphoreType.DMA((PIECES,))
     return pl.pallas_call(
         finish_kernel,
         out_shape=(
             jax.ShapeDtypeStruct((rows, dims), jnp.bfloat16),
             jax.ShapeDtypeStruct((rows, cols), jnp.float32),
         ),
-        in_specs=[SMEM, VMEM, VMEM, ANY, ANY],
-        out_specs=(ANY, VMEM),
+        in_specs=[SMEM, VMEM, VMEM, HBM, HBM],
+        out_specs=(HBM, VMEM),
         scratch_shapes=[
             pltpu.VMEM(half.shape, half.dtype),
             pltpu.VMEM(half.shape, half.dtype),
@@ -181,13 +221,13 @@
     shards = lax.axis_size("z")
     peers = lax.axis_size("param")
     core = lax.axis_index("core").astype(jnp.int32)[None]
-    other_p = swap_cores(particles)
-    other_s = swap_cores(scores)
-    packed, other_p, other_s = lax.optimization_barrier((packed_shard(basis), other_p, other_s))
-    gathered = lax.all_gather(packed, "z", axis=0, tiled=True)
+    theirs, packed = prepare(core, particles, scores, basis)
+    others = swap_cores(theirs)
+    gathered = lax.all_gather(packed.astype(jnp.float16), "z", axis=0, tiled=True)
     half = unpacked(gathered, shards)
-    other_half = swap_cores(half)
-    pair = contract(core, particles, scores, other_p, other_s, half)
+    pair = contract(core, particles, scores, others, half)
+    pair, held = lax.optimization_barrier((pair, half))
+    other_half = swap_cores(held)
     pieces = jnp.broadcast_to(pair[None], (peers, *pair.shape)).reshape(2 * peers, rows, -1)
     summed = lax.all_to_all(pieces, ("param", "core"), 0, 0, tiled=True).sum(axis=0)
     column = sent_to_all(summed, "z").reshape(shards * rows, -1)

time: 141 us -> 137 us (0.972)
  Pallas kernels: 8.9 us -> 12 us
  starting transfers between devices: 19.1 us -> 16.6 us
  local copies, waits for them, and re-layouts: 2.32 us -> 0.08 us
  other arithmetic: 5.93 us -> 4.32 us
    pallas_call x0 -> x1, Pallas kernels: none -> 2.98 us  [prepare(): pl.pallas_call(prepare_kernel, out_shape=(jax.ShapeDtypeStruct((2 * rows,...]
    ppermute x3 -> x2, starting transfers between devices: 19.1 us -> 16.6 us  [swap_cores(): return lax.ppermute(array, 'core', [(0, 1), (1, 0)])]
    unnamed x8 -> x4, local copies, waits for them, and re-layouts: 2.19 us -> 0.01 us
    reduce_max x1 -> x0, other arithmetic: 1.59 us -> none  [packed_shard(): largest = jnp.maximum(jnp.max(jnp.abs(wide)), 1e-30)]
  transfers between devices with their start and end apart: 3 -> 2, of which waited for: 0 -> 0; matrix products, arithmetic and copies ran while one was open for 2% -> 3% of each run, Pallas kernels for 2% -> 0%
where the time goes in v3:
time: 137 us; the launch traced here: 136 us
  blocking collectives  103 us (75%)
  starting transfers between devices  16.6 us (12%)
  Pallas kernels  12 us (9%)
  other arithmetic  4.32 us (3%)
    all_gather x1, blocking collectives, body(): lax.all_gather(packed.astype(jnp.float16), 'z', axis=0, tiled=True)  56.2 us
    all_to_all x1, blocking collectives, sent_to_all(): lax.all_to_all(jnp.broadcast_to(array[None], (peers, *array.shape)), axis...  20.8 us
    all_to_all x1, blocking collectives, body(): lax.all_to_all(pieces, ('param', 'core'), 0, 0, tiled=True).sum(axis=0)  18.6 us
    ppermute x2, starting transfers between devices, swap_cores(): return lax.ppermute(array, 'core', [(0, 1), (1, 0)])  16.6 us
    all_gather x1, blocking collectives, body(): everyone = lax.all_gather(column, 'core', axis=0, tiled=True)  7.16 us
    pallas_call x1, Pallas kernels, finish(): pl.pallas_call(finish_kernel, out_shape=(jax.ShapeDtypeStruct((rows, dims...  6.51 us
    convert_element_type x1, other arithmetic, unpacked(): return wide.astype(jnp.bfloat16)  3.06 us
    pallas_call x1, Pallas kernels, prepare(): pl.pallas_call(prepare_kernel, out_shape=(jax.ShapeDtypeStruct((2 * rows,...  2.98 us
  transfers between devices with their start and end apart: 2, of which 0 were waited for; matrix products, arithmetic and copies ran while one was open for 3% of the time, Pallas kernels for 0%

profile of v3, /device:TPU:1, one launch (start us, length us, event | category | flops | bytes accessed | tf_op | source)
XLA Modules:
  0.0 136.3 jit_solution(11091977863510508318)
XLA Ops:
  0.6 3.0 %shard_map.50 = (bf16[32,16384]{1,0:T(8,128)(2,1)}, bf16[1040,128]{1,0:T(8,128)(2,1)}) custom-call(s32[1]{0:T(128)} %bitcast.core_ref, bf16[16,32768]{1,0:T(8,128)(2,1)} %p_ref.1, bf16[16,32768]{1,0:T(8,128)(2,1)} %s_ref.1, bf16[1024,128]{1,0:T(8,128)(2,1)} %basis_hbm.1), custom_call_target="tpu_custom_call" | custom-call | flops 262144 | bytes 2097152 | tf_op jit(solution)/shard_map/pallas_call | solution.py:56
  3.6 8.8 %collective-permute-start = (bf16[32,16384]{1,0:T(8,128)(2,1)}, bf16[32,16384]{1,0:T(8,128)(2,1)S(1)}, u32[]{:S(2)}, u32[]{:S(2)}) collective-permute-start(bf16[32,16384]{1,0:T(8,128)(2,1)} %get-tuple-element.6), channel_id=1, source_target_pairs={{0,1},{1,0},{2,3},{3,2},{4,5},{5,4},{6,7},{7,6},{8,9},{9,8},{10,11... | collective-permute-start | bytes 3145736 | tf_op jit(solution)/shard_map/ppermute | solution.py:24
  12.4 1.0 convert_element_type.10
  13.4 56.2 %all-gather.1 = f16[16640,128]{1,0:T(8,128)(2,1)S(1)} all-gather(f16[1040,128]{1,0:T(8,128)(2,1)S(1)} %convert_element_type.10), channel_id=1, replica_groups=mesh['param'=16,'z'=16,'core'=2] {'z'}, dimensions={0}, use_global_device_ids=true | all-gather | bytes 4526080 | tf_op jit(solution)/shard_map/all_gather | solution.py:226
  69.6 0.0 copy-start
  69.6 0.0 copy-start.1
  69.6 0.2 fusion.3
  69.8 3.1 %multiply_convert_fusion.half_hbm = bf16[16,1024,128]{2,1,0:T(8,128)(2,1)} fusion(f16[16,1040,128]{2,1,0:T(8,128)(2,1)S(1)} %bitcast.5, f32[16]{0:T(128)S(1)} %fusion.3), kind=kLoop, calls=%fused_computation | loop fusion | flops 6291456 | bytes 8388672 | tf_op jit(solution)/shard_map/convert_element_type | solution.py:79
  72.9 0.0 collective-permute-done.others_ref
  72.9 0.0 copy-done
  72.9 0.0 copy-done.1
  72.9 2.5 %shard_map.51 = f32[2,16,256]{2,1,0:T(8,128)S(1)} custom-call(s32[1]{0:T(128)} %bitcast.core_ref, bf16[16,32768]{1,0:T(8,128)(2,1)S(1)} %copy-done, bf16[16,32768]{1,0:T(8,128)(2,1)S(1)} %copy-done.1, bf16[32,16384]{1,0:T(8,128)(2,1)S(1)} %collective-permute-done.others_ref, bf16[16,1024,128]{2,1,0:T(8,128)(2,1)} %multiply_convert_fusion.half_hbm), custom_call_target="tpu_custom_call" | custom-call | flops 268435456 | bytes 4194304 | tf_op jit(solution)/shard_map/pallas_call | solution.py:116
  75.4 7.8 %collective-permute-start.1 = (bf16[16,1024,128]{2,1,0:T(8,128)(2,1)}, bf16[16,1024,128]{2,1,0:T(8,128)(2,1)}, u32[]{:S(2)}, u32[]{:S(2)}) collective-permute-start(bf16[16,1024,128]{2,1,0:T(8,128)(2,1)} %multiply_convert_fusion.half_hbm), channel_id=1, source_target_pairs={{0,1},{1,0},{2,3},{3,2},{4,5},{5,4},{6,7},{7,6},{8,9},{9,8},{10,11... | collective-permute-start | bytes 12582920 | tf_op jit(solution)/shard_map/ppermute | solution.py:24
  83.2 0.1 broadcast_in_dim.7
  83.3 18.6 %all_to_all.10 = f32[32,16,256]{2,1,0:T(8,128)S(1)} all-to-all(f32[32,16,256]{2,1,0:T(8,128)S(1)} %bitcast.6), channel_id=1, replica_groups=mesh['param'=16,'z'=16,'core'=2] {'param','core'}, dimensions={0} | all-to-all | bytes 1048576 | tf_op jit(solution)/shard_map/all_to_all | solution.py:232
  101.9 20.8 %all_to_all.11 = f32[16,16,256]{2,1,0:T(8,128)S(1)} all-to-all(f32[16,16,256]{2,1,0:T(8,128)S(1)} %broadcast_in_dim.8), channel_id=1, replica_groups=mesh['param'=16,'z'=16,'core'=2] {'z'}, dimensions={0} | all-to-all | bytes 524288 | tf_op jit(solution)/shard_map/all_to_all | solution.py:214
  122.7 7.2 %all_gather.7.every_ref = f32[512,256]{1,0:T(8,128)S(1)} all-gather(f32[256,256]{1,0:T(8,128)S(1)} %bitcast.7), channel_id=1, replica_groups=mesh['param'=16,'z'=16,'core'=2] {'core'}, dimensions={0}, use_global_device_ids=true | all-gather | bytes 786432 | tf_op jit(solution)/shard_map/all_gather | solution.py:234
  129.8 0.0 collective-permute-done.1.other_hbm
  129.8 6.5 %shard_map.52 = (bf16[16,32768]{1,0:T(8,128)(2,1)}, f32[16,128]{1,0:T(8,128)}) custom-call(s32[1]{0:T(128)} %bitcast.core_ref, f32[16,256]{1,0:T(8,128)S(1)} %reduce_sum.9.own_ref, f32[512,256]{1,0:T(8,128)S(1)} %all_gather.7.every_ref, bf16[16,1024,128]{2,1,0:T(8,128)(2,1)} %multiply_convert_fusion.half_hbm, ...), custom_call_target="tpu_custom_call" | custom-call | flops 134217728 | bytes 8388608 | tf_op jit(solution)/shard_map/pallas_call | solution.py:189
  (2 shorter events, 0.1 us)
Async XLA Ops:
  3.6 69.2 %collective-permute-start = (bf16[32,16384]{1,0:T(8,128)(2,1)}, bf16[32,16384]{1,0:T(8,128)(2,1)S(1)}, u32[]{:S(2)}, u32[]{:S(2)}) collective-permute-start(bf16[32,16384]{1,0:T(8,128)(2,1)} %get-tuple-element.6), channel_id=1, source_target_pairs={{0,1},{1,0},{2,3},{3,2},{4,5},{5,4},{6,7},{7,6},{8,9},{9,8},{10,11... | collective-permute-start | bytes 3145736 | tf_op jit(solution)/shard_map/ppermute | solution.py:24
  69.6 3.3 %copy-start = (bf16[16,32768]{1,0:T(8,128)(2,1)S(1)}, bf16[16,32768]{1,0:T(8,128)(2,1)}, u32[]{:S(2)}) copy-start(bf16[16,32768]{1,0:T(8,128)(2,1)} %p_ref.1) | copy-start | bytes 3145732
  69.6 3.3 %copy-start.1 = (bf16[16,32768]{1,0:T(8,128)(2,1)S(1)}, bf16[16,32768]{1,0:T(8,128)(2,1)}, u32[]{:S(2)}) copy-start(bf16[16,32768]{1,0:T(8,128)(2,1)} %s_ref.1) | copy-start | bytes 3145732
  75.4 54.4 %collective-permute-start.1 = (bf16[16,1024,128]{2,1,0:T(8,128)(2,1)}, bf16[16,1024,128]{2,1,0:T(8,128)(2,1)}, u32[]{:S(2)}, u32[]{:S(2)}) collective-permute-start(bf16[16,1024,128]{2,1,0:T(8,128)(2,1)} %multiply_convert_fusion.half_hbm), channel_id=1, source_target_pairs={{0,1},{1,0},{2,3},{3,2},{4,5},{5,4},{6,7},{7,6},{8,9},{9,8},{10,11... | collective-permute-start | bytes 12582920 | tf_op jit(solution)/shard_map/ppermute | solution.py:24

commit v4 on v3

--- a/solution.py
+++ b/solution.py
@@ -90,17 +90,15 @@
     ]
 
 
-def contract_kernel(core_ref, p_ref, s_ref, others_ref, half_hbm, out_ref, half_ref, sems):
+def contract_kernel(core_ref, p_ref, s_ref, others_ref, half_ref, out_ref, kept_hbm, sems):
     core = core_ref[0]
     shards, depth, cols = half_ref.shape
     rows = p_ref.shape[0]
-    copies = chunk_copies(half_hbm, half_ref, sems)
+    copies = chunk_copies(half_ref, kept_hbm, sems)
     for copy in copies:
         copy.start()
     total = jnp.zeros((4 * rows, cols), jnp.float32)
     for i in range(shards):
-        if i % (shards // CHUNKS) == 0:
-            copies[i // (shards // CHUNKS)].wait()
         at = pl.ds(pl.multiple_of((2 * i + core) * depth, depth), depth)
         theirs = others_ref[:, i * depth : (i + 1) * depth]
         block = jnp.concatenate([p_ref[:, at], s_ref[:, at], theirs], axis=0)
@@ -109,16 +107,21 @@
     other = jnp.concatenate([total[2 * rows : 3 * rows], total[3 * rows :]], axis=1)
     out_ref[core] = own
     out_ref[1 - core] = other
+    for copy in copies:
+        copy.wait()
 
 
 def contract(core, particles, scores, others, half):
     rows, cols = particles.shape[0], half.shape[2]
     return pl.pallas_call(
         contract_kernel,
-        out_shape=jax.ShapeDtypeStruct((2, rows, 2 * cols), jnp.float32),
-        in_specs=[SMEM] + [VMEM] * 3 + [HBM],
-        out_specs=VMEM,
-        scratch_shapes=[pltpu.VMEM(half.shape, half.dtype), pltpu.SemaphoreType.DMA((CHUNKS,))],
+        out_shape=(
+            jax.ShapeDtypeStruct((2, rows, 2 * cols), jnp.float32),
+            jax.ShapeDtypeStruct(half.shape, half.dtype),
+        ),
+        in_specs=[SMEM] + [VMEM] * 4,
+        out_specs=(VMEM, HBM),
+        scratch_shapes=[pltpu.SemaphoreType.DMA((CHUNKS,))],
         compiler_params=pltpu.CompilerParams(vmem_limit_bytes=24 << 20),
         cost_estimate=pl.CostEstimate(
             flops=2 * 4 * rows * half.size, bytes_accessed=2 * half.size, transcendentals=0
@@ -224,10 +227,8 @@
     theirs, packed = prepare(core, particles, scores, basis)
     others = swap_cores(theirs)
     gathered = lax.all_gather(packed.astype(jnp.float16), "z", axis=0, tiled=True)
-    half = unpacked(gathered, shards)
-    pair = contract(core, particles, scores, others, half)
-    pair, held = lax.optimization_barrier((pair, half))
-    other_half = swap_cores(held)
+    pair, half = contract(core, particles, scores, others, unpacked(gathered, shards))
+    other_half = swap_cores(half)
     pieces = jnp.broadcast_to(pair[None], (peers, *pair.shape)).reshape(2 * peers, rows, -1)
     summed = lax.all_to_all(pieces, ("param", "core"), 0, 0, tiled=True).sum(axis=0)
     column = sent_to_all(summed, "z").reshape(shards * rows, -1)

time: 137 us -> 135 us (0.985)
  other arithmetic: 4.32 us -> 2.39 us
    convert_element_type x1, other arithmetic: 3.06 us -> 1.13 us  [unpacked(): return wide.astype(jnp.bfloat16)]
  transfers between devices with their start and end apart: 2 -> 2, of which waited for: 0 -> 0; matrix products, arithmetic and copies ran while one was open for 3% -> 2% of each run, Pallas kernels for 0% -> 0%
where the time goes in v4:
time: 135 us; the launch traced here: 134 us
  blocking collectives  103 us (76%)
  starting transfers between devices  16.6 us (12%)
  Pallas kernels  11.8 us (9%)
  other arithmetic  2.39 us (2%)
    all_gather x1, blocking collectives, body(): lax.all_gather(packed.astype(jnp.float16), 'z', axis=0, tiled=True)  56.2 us
    all_to_all x1, blocking collectives, sent_to_all(): lax.all_to_all(jnp.broadcast_to(array[None], (peers, *array.shape)), axis...  20.8 us
    all_to_all x1, blocking collectives, body(): lax.all_to_all(pieces, ('param', 'core'), 0, 0, tiled=True).sum(axis=0)  18.6 us
    ppermute x2, starting transfers between devices, swap_cores(): return lax.ppermute(array, 'core', [(0, 1), (1, 0)])  16.6 us
    all_gather x1, blocking collectives, body(): everyone = lax.all_gather(column, 'core', axis=0, tiled=True)  7.16 us
    pallas_call x1, Pallas kernels, finish(): pl.pallas_call(finish_kernel, out_shape=(jax.ShapeDtypeStruct((rows, dims...  6.51 us
    pallas_call x1, Pallas kernels, prepare(): pl.pallas_call(prepare_kernel, out_shape=(jax.ShapeDtypeStruct((2 * rows,...  2.97 us
  transfers between devices with their start and end apart: 2, of which 0 were waited for; matrix products, arithmetic and copies ran while one was open for 2% of the time, Pallas kernels for 0%

profile of v4, /device:TPU:1, one launch (start us, length us, event | category | flops | bytes accessed | tf_op | source)
XLA Modules:
  0.0 134.4 jit_solution(13576130532496607971)
XLA Ops:
  0.6 3.0 %shard_map.50 = (bf16[32,16384]{1,0:T(8,128)(2,1)}, bf16[1040,128]{1,0:T(8,128)(2,1)}) custom-call(s32[1]{0:T(128)} %bitcast.core_ref, bf16[16,32768]{1,0:T(8,128)(2,1)} %p_ref.1, bf16[16,32768]{1,0:T(8,128)(2,1)} %s_ref.1, bf16[1024,128]{1,0:T(8,128)(2,1)} %basis_hbm.1), custom_call_target="tpu_custom_call" | custom-call | flops 262144 | bytes 2097152 | tf_op jit(solution)/shard_map/pallas_call | solution.py:56
  3.6 8.8 %collective-permute-start = (bf16[32,16384]{1,0:T(8,128)(2,1)}, bf16[32,16384]{1,0:T(8,128)(2,1)S(1)}, u32[]{:S(2)}, u32[]{:S(2)}) collective-permute-start(bf16[32,16384]{1,0:T(8,128)(2,1)} %get-tuple-element.6), channel_id=1, source_target_pairs={{0,1},{1,0},{2,3},{3,2},{4,5},{5,4},{6,7},{7,6},{8,9},{9,8},{10,11... | collective-permute-start | bytes 3145736 | tf_op jit(solution)/shard_map/ppermute | solution.py:24
  12.4 1.0 convert_element_type.10
  13.4 56.2 %all-gather.1 = f16[16640,128]{1,0:T(8,128)(2,1)S(1)} all-gather(f16[1040,128]{1,0:T(8,128)(2,1)S(1)} %convert_element_type.10), channel_id=1, replica_groups=mesh['param'=16,'z'=16,'core'=2] {'z'}, dimensions={0}, use_global_device_ids=true | all-gather | bytes 4526080 | tf_op jit(solution)/shard_map/all_gather | solution.py:229
  69.6 0.0 copy-start
  69.6 0.0 copy-start.1
  69.6 0.2 fusion.3
  69.8 1.1 multiply_convert_fusion.half_ref
  70.9 0.0 collective-permute-done.others_ref
  70.9 0.0 copy-done
  70.9 0.2 copy-done.1
  71.1 2.3 %shard_map.51 = (f32[2,16,256]{2,1,0:T(8,128)S(1)}, bf16[16,1024,128]{2,1,0:T(8,128)(2,1)}) custom-call(s32[1]{0:T(128)} %bitcast.core_ref, bf16[16,32768]{1,0:T(8,128)(2,1)S(1)} %copy-done, bf16[16,32768]{1,0:T(8,128)(2,1)S(1)} %copy-done.1, bf16[32,16384]{1,0:T(8,128)(2,1)S(1)} %collective-permute-done.others_ref, ...), custom_call_target="tpu_custom_call" | custom-call | flops 268435456 | bytes 4194304 | tf_op jit(solution)/shard_map/pallas_call | solution.py:116
  73.4 7.8 %collective-permute-start.1 = (bf16[16,1024,128]{2,1,0:T(8,128)(2,1)}, bf16[16,1024,128]{2,1,0:T(8,128)(2,1)}, u32[]{:S(2)}, u32[]{:S(2)}) collective-permute-start(bf16[16,1024,128]{2,1,0:T(8,128)(2,1)} %get-tuple-element.9.half_hbm), channel_id=1, source_target_pairs={{0,1},{1,0},{2,3},{3,2},{4,5},{5,4},{6,7},{7,6},{8,9},{9,8},{10,11... | collective-permute-start | bytes 12582920 | tf_op jit(solution)/shard_map/ppermute | solution.py:24
  81.2 0.1 broadcast_in_dim.7
  81.3 18.6 %all_to_all.10 = f32[32,16,256]{2,1,0:T(8,128)S(1)} all-to-all(f32[32,16,256]{2,1,0:T(8,128)S(1)} %bitcast.6), channel_id=1, replica_groups=mesh['param'=16,'z'=16,'core'=2] {'param','core'}, dimensions={0} | all-to-all | bytes 1048576 | tf_op jit(solution)/shard_map/all_to_all | solution.py:233
  99.9 20.8 %all_to_all.11 = f32[16,16,256]{2,1,0:T(8,128)S(1)} all-to-all(f32[16,16,256]{2,1,0:T(8,128)S(1)} %broadcast_in_dim.8), channel_id=1, replica_groups=mesh['param'=16,'z'=16,'core'=2] {'z'}, dimensions={0} | all-to-all | bytes 524288 | tf_op jit(solution)/shard_map/all_to_all | solution.py:217
  120.7 7.2 %all_gather.7.every_ref = f32[512,256]{1,0:T(8,128)S(1)} all-gather(f32[256,256]{1,0:T(8,128)S(1)} %bitcast.7), channel_id=1, replica_groups=mesh['param'=16,'z'=16,'core'=2] {'core'}, dimensions={0}, use_global_device_ids=true | all-gather | bytes 786432 | tf_op jit(solution)/shard_map/all_gather | solution.py:235
  127.8 0.0 collective-permute-done.1.other_hbm
  127.8 6.5 %shard_map.52 = (bf16[16,32768]{1,0:T(8,128)(2,1)}, f32[16,128]{1,0:T(8,128)}) custom-call(s32[1]{0:T(128)} %bitcast.core_ref, f32[16,256]{1,0:T(8,128)S(1)} %reduce_sum.9.own_ref, f32[512,256]{1,0:T(8,128)S(1)} %all_gather.7.every_ref, bf16[16,1024,128]{2,1,0:T(8,128)(2,1)} %get-tuple-element.9.half_hbm, bf16[16,1024,128]{2,1,0:T(8,128)(2,1)} %collective-permute-done.1.other_hbm), custom_call_target="tpu_custom_call" | custom-call | flops 134217728 | bytes 8388608 | tf_op jit(solution)/shard_map/pallas_call | solution.py:192
  (2 shorter events, 0.1 us)
Async XLA Ops:
  3.6 67.3 %collective-permute-start = (bf16[32,16384]{1,0:T(8,128)(2,1)}, bf16[32,16384]{1,0:T(8,128)(2,1)S(1)}, u32[]{:S(2)}, u32[]{:S(2)}) collective-permute-start(bf16[32,16384]{1,0:T(8,128)(2,1)} %get-tuple-element.6), channel_id=1, source_target_pairs={{0,1},{1,0},{2,3},{3,2},{4,5},{5,4},{6,7},{7,6},{8,9},{9,8},{10,11... | collective-permute-start | bytes 3145736 | tf_op jit(solution)/shard_map/ppermute | solution.py:24
  69.6 1.4 %copy-start = (bf16[16,32768]{1,0:T(8,128)(2,1)S(1)}, bf16[16,32768]{1,0:T(8,128)(2,1)}, u32[]{:S(2)}) copy-start(bf16[16,32768]{1,0:T(8,128)(2,1)} %p_ref.1) | copy-start | bytes 3145732
  69.6 1.5 %copy-start.1 = (bf16[16,32768]{1,0:T(8,128)(2,1)S(1)}, bf16[16,32768]{1,0:T(8,128)(2,1)}, u32[]{:S(2)}) copy-start(bf16[16,32768]{1,0:T(8,128)(2,1)} %s_ref.1) | copy-start | bytes 3145732
  73.4 54.4 %collective-permute-start.1 = (bf16[16,1024,128]{2,1,0:T(8,128)(2,1)}, bf16[16,1024,128]{2,1,0:T(8,128)(2,1)}, u32[]{:S(2)}, u32[]{:S(2)}) collective-permute-start(bf16[16,1024,128]{2,1,0:T(8,128)(2,1)} %get-tuple-element.9.half_hbm), channel_id=1, source_target_pairs={{0,1},{1,0},{2,3},{3,2},{4,5},{5,4},{6,7},{7,6},{8,9},{9,8},{10,11... | collective-permute-start | bytes 12582920 | tf_op jit(solution)/shard_map/ppermute | solution.py:24

commit v5 on v4

--- a/solution.py
+++ b/solution.py
@@ -25,7 +25,8 @@
 
 
 def prepare_kernel(
-    core_ref, p_hbm, s_hbm, basis_hbm, theirs_ref, packed_ref, basis_ref, sems, basis_sem
+    core_ref, p_hbm, s_hbm, basis_hbm, theirs_hbm, packed_ref,
+    basis_ref, theirs_ref, sems, basis_sem, out_sems,
 ):
     core = core_ref[0]
     rows = p_hbm.shape[0]
@@ -40,14 +41,22 @@
             copies.append(pltpu.make_async_copy(source.at[:, at], target, sems.at[k, i]))
     for copy in copies:
         copy.start()
+    outs = []
+    for k in range(2):
+        for copy in copies[k * len(copies) // 2 : (k + 1) * len(copies) // 2]:
+            copy.wait()
+        part = pl.ds(k * rows, rows)
+        out = pltpu.make_async_copy(theirs_ref.at[part], theirs_hbm.at[part], out_sems.at[k])
+        out.start()
+        outs.append(out)
     fetch.wait()
     wide = basis_ref[...].astype(jnp.float32)
     largest = jnp.max(jnp.max(jnp.abs(wide), axis=0, keepdims=True), axis=1, keepdims=True)
     power = jnp.ceil(jnp.log2(jnp.maximum(largest, 1e-30)))
     packed_ref[:depth] = (wide * jnp.exp2(TOP - power)).astype(jnp.bfloat16)
     packed_ref[depth:] = jnp.broadcast_to(power, (TAIL, wide.shape[1])).astype(jnp.bfloat16)
-    for copy in copies:
-        copy.wait()
+    for out in outs:
+        out.wait()
 
 
 def prepare(core, particles, scores, basis):
@@ -60,11 +69,13 @@
             jax.ShapeDtypeStruct((depth + TAIL, basis.shape[1]), jnp.bfloat16),
         ),
         in_specs=[SMEM, HBM, HBM, HBM],
-        out_specs=(VMEM, VMEM),
+        out_specs=(HBM, VMEM),
         scratch_shapes=[
             pltpu.VMEM(basis.shape, basis.dtype),
+            pltpu.VMEM((2 * rows, cols // 2), particles.dtype),
             pltpu.SemaphoreType.DMA((2, cols // 2 // depth)),
             pltpu.SemaphoreType.DMA,
+            pltpu.SemaphoreType.DMA((2,)),
         ],
         cost_estimate=pl.CostEstimate(
             flops=2 * basis.size, bytes_accessed=4 * particles.size, transcendentals=0
@@ -148,8 +159,8 @@
 
 
 def finish_kernel(
-    core_ref, own_ref, every_ref, half_hbm, other_hbm, velocity_hbm, phi_ref,
-    half_ref, other_ref, velocity_ref, half_sems, other_sems, out_sems,
+    core_ref, own_ref, every_ref, half_hbm, other_hbm, velocity_hbm, phi_hbm,
+    half_ref, other_ref, velocity_ref, phi_ref, half_sems, other_sems, out_sems, phi_sem,
 ):
     core = core_ref[0]
     shards, depth, cols = half_ref.shape
@@ -164,11 +175,13 @@
             copy.start()
     phi = stein_terms(own_ref[:, :cols], every_ref[...])
     phi_ref[...] = phi
+    phi_out = pltpu.make_async_copy(phi_ref, phi_hbm, phi_sem)
+    phi_out.start()
     low = phi.astype(jnp.bfloat16)
     scale = math.sqrt(P_SIZE / R)
     each = shards // PIECES
     span = 2 * each * depth
-    outs = []
+    outs = [phi_out]
     for k in range(PIECES):
         for copy in copies[k]:
             copy.wait()
@@ -196,14 +209,16 @@
             jax.ShapeDtypeStruct((rows, cols), jnp.float32),
         ),
         in_specs=[SMEM, VMEM, VMEM, HBM, HBM],
-        out_specs=(HBM, VMEM),
+        out_specs=(HBM, HBM),
         scratch_shapes=[
             pltpu.VMEM(half.shape, half.dtype),
             pltpu.VMEM(half.shape, half.dtype),
             pltpu.VMEM((rows, dims), jnp.bfloat16),
+            pltpu.VMEM((rows, cols), jnp.float32),
             sems,
             sems,
             sems,
+            pltpu.SemaphoreType.DMA,
         ],
         compiler_params=pltpu.CompilerParams(vmem_limit_bytes=24 << 20),
         cost_estimate=pl.CostEstimate(

time: 135 us -> 134 us (level)
  no operation moved by 1% of the time
where the time goes in v5:
time: 134 us
  blocking collectives  103 us (77%)
  starting transfers between devices  16.6 us (12%)
  Pallas kernels  11.2 us (8%)
  other arithmetic  2.39 us (2%)
    all_gather x1, blocking collectives, body(): lax.all_gather(packed.astype(jnp.float16), 'z', axis=0, tiled=True)  56.2 us
    all_to_all x1, blocking collectives, sent_to_all(): lax.all_to_all(jnp.broadcast_to(array[None], (peers, *array.shape)), axis...  20.8 us
    all_to_all x1, blocking collectives, body(): lax.all_to_all(pieces, ('param', 'core'), 0, 0, tiled=True).sum(axis=0)  18.6 us
    ppermute x2, starting transfers between devices, swap_cores(): return lax.ppermute(array, 'core', [(0, 1), (1, 0)])  16.6 us
    all_gather x1, blocking collectives, body(): everyone = lax.all_gather(column, 'core', axis=0, tiled=True)  7.16 us
    pallas_call x1, Pallas kernels, finish(): pl.pallas_call(finish_kernel, out_shape=(jax.ShapeDtypeStruct((rows, dims...  5.92 us
    pallas_call x1, Pallas kernels, prepare(): pl.pallas_call(prepare_kernel, out_shape=(jax.ShapeDtypeStruct((2 * rows,...  2.98 us
  transfers between devices with their start and end apart: 2, of which 0 were waited for; matrix products, arithmetic and copies ran while one was open for 2% of the time, Pallas kernels for 0%

profile of v5, /device:TPU:1, one launch (start us, length us, event | category | flops | bytes accessed | tf_op | source)
XLA Modules:
  0.0 133.8 jit_solution(1467928081483799905)
XLA Ops:
  0.6 3.0 %shard_map.50 = (bf16[32,16384]{1,0:T(8,128)(2,1)}, bf16[1040,128]{1,0:T(8,128)(2,1)}) custom-call(s32[1]{0:T(128)} %bitcast.core_ref, bf16[16,32768]{1,0:T(8,128)(2,1)} %p_ref.1, bf16[16,32768]{1,0:T(8,128)(2,1)} %s_ref.1, bf16[1024,128]{1,0:T(8,128)(2,1)} %basis_hbm.1), custom_call_target="tpu_custom_call" | custom-call | flops 262144 | bytes 2097152 | tf_op jit(solution)/shard_map/pallas_call | solution.py:65
  3.6 8.8 %collective-permute-start = (bf16[32,16384]{1,0:T(8,128)(2,1)}, bf16[32,16384]{1,0:T(8,128)(2,1)S(1)}, u32[]{:S(2)}, u32[]{:S(2)}) collective-permute-start(bf16[32,16384]{1,0:T(8,128)(2,1)} %get-tuple-element.6), channel_id=1, source_target_pairs={{0,1},{1,0},{2,3},{3,2},{4,5},{5,4},{6,7},{7,6},{8,9},{9,8},{10,11... | collective-permute-start | bytes 3145736 | tf_op jit(solution)/shard_map/ppermute | solution.py:24
  12.4 1.0 convert_element_type.10
  13.4 56.2 %all-gather.1 = f16[16640,128]{1,0:T(8,128)(2,1)S(1)} all-gather(f16[1040,128]{1,0:T(8,128)(2,1)S(1)} %convert_element_type.10), channel_id=1, replica_groups=mesh['param'=16,'z'=16,'core'=2] {'z'}, dimensions={0}, use_global_device_ids=true | all-gather | bytes 4526080 | tf_op jit(solution)/shard_map/all_gather | solution.py:244
  69.6 0.0 copy-start
  69.6 0.0 copy-start.1
  69.6 0.2 fusion.3
  69.8 1.1 multiply_convert_fusion.half_ref
  70.9 0.0 collective-permute-done.others_ref
  70.9 0.0 copy-done
  70.9 0.2 copy-done.1
  71.1 2.3 %shard_map.51 = (f32[2,16,256]{2,1,0:T(8,128)S(1)}, bf16[16,1024,128]{2,1,0:T(8,128)(2,1)}) custom-call(s32[1]{0:T(128)} %bitcast.core_ref, bf16[16,32768]{1,0:T(8,128)(2,1)S(1)} %copy-done, bf16[16,32768]{1,0:T(8,128)(2,1)S(1)} %copy-done.1, bf16[32,16384]{1,0:T(8,128)(2,1)S(1)} %collective-permute-done.others_ref, ...), custom_call_target="tpu_custom_call" | custom-call | flops 268435456 | bytes 4194304 | tf_op jit(solution)/shard_map/pallas_call | solution.py:127
  73.4 7.8 %collective-permute-start.1 = (bf16[16,1024,128]{2,1,0:T(8,128)(2,1)}, bf16[16,1024,128]{2,1,0:T(8,128)(2,1)}, u32[]{:S(2)}, u32[]{:S(2)}) collective-permute-start(bf16[16,1024,128]{2,1,0:T(8,128)(2,1)} %get-tuple-element.9.half_hbm), channel_id=1, source_target_pairs={{0,1},{1,0},{2,3},{3,2},{4,5},{5,4},{6,7},{7,6},{8,9},{9,8},{10,11... | collective-permute-start | bytes 12582920 | tf_op jit(solution)/shard_map/ppermute | solution.py:24
  81.2 0.1 broadcast_in_dim.7
  81.3 18.6 %all_to_all.10 = f32[32,16,256]{2,1,0:T(8,128)S(1)} all-to-all(f32[32,16,256]{2,1,0:T(8,128)S(1)} %bitcast.6), channel_id=1, replica_groups=mesh['param'=16,'z'=16,'core'=2] {'param','core'}, dimensions={0} | all-to-all | bytes 1048576 | tf_op jit(solution)/shard_map/all_to_all | solution.py:248
  99.9 20.8 %all_to_all.11 = f32[16,16,256]{2,1,0:T(8,128)S(1)} all-to-all(f32[16,16,256]{2,1,0:T(8,128)S(1)} %broadcast_in_dim.8), channel_id=1, replica_groups=mesh['param'=16,'z'=16,'core'=2] {'z'}, dimensions={0} | all-to-all | bytes 524288 | tf_op jit(solution)/shard_map/all_to_all | solution.py:232
  120.7 7.2 %all_gather.7.every_ref = f32[512,256]{1,0:T(8,128)S(1)} all-gather(f32[256,256]{1,0:T(8,128)S(1)} %bitcast.7), channel_id=1, replica_groups=mesh['param'=16,'z'=16,'core'=2] {'core'}, dimensions={0}, use_global_device_ids=true | all-gather | bytes 786432 | tf_op jit(solution)/shard_map/all_gather | solution.py:250
  127.8 0.0 collective-permute-done.1.other_hbm
  127.8 5.9 %shard_map.52 = (bf16[16,32768]{1,0:T(8,128)(2,1)}, f32[16,128]{1,0:T(8,128)}) custom-call(s32[1]{0:T(128)} %bitcast.core_ref, f32[16,256]{1,0:T(8,128)S(1)} %reduce_sum.9.own_ref, f32[512,256]{1,0:T(8,128)S(1)} %all_gather.7.every_ref, bf16[16,1024,128]{2,1,0:T(8,128)(2,1)} %get-tuple-element.9.half_hbm, bf16[16,1024,128]{2,1,0:T(8,128)(2,1)} %collective-permute-done.1.other_hbm), custom_call_target="tpu_custom_call" | custom-call | flops 134217728 | bytes 8388608 | tf_op jit(solution)/shard_map/pallas_call | solution.py:205
  (2 shorter events, 0.1 us)
Async XLA Ops:
  3.6 67.3 %collective-permute-start = (bf16[32,16384]{1,0:T(8,128)(2,1)}, bf16[32,16384]{1,0:T(8,128)(2,1)S(1)}, u32[]{:S(2)}, u32[]{:S(2)}) collective-permute-start(bf16[32,16384]{1,0:T(8,128)(2,1)} %get-tuple-element.6), channel_id=1, source_target_pairs={{0,1},{1,0},{2,3},{3,2},{4,5},{5,4},{6,7},{7,6},{8,9},{9,8},{10,11... | collective-permute-start | bytes 3145736 | tf_op jit(solution)/shard_map/ppermute | solution.py:24
  69.6 1.4 %copy-start = (bf16[16,32768]{1,0:T(8,128)(2,1)S(1)}, bf16[16,32768]{1,0:T(8,128)(2,1)}, u32[]{:S(2)}) copy-start(bf16[16,32768]{1,0:T(8,128)(2,1)} %p_ref.1) | copy-start | bytes 3145732
  69.6 1.5 %copy-start.1 = (bf16[16,32768]{1,0:T(8,128)(2,1)S(1)}, bf16[16,32768]{1,0:T(8,128)(2,1)}, u32[]{:S(2)}) copy-start(bf16[16,32768]{1,0:T(8,128)(2,1)} %s_ref.1) | copy-start | bytes 3145732
  73.4 54.4 %collective-permute-start.1 = (bf16[16,1024,128]{2,1,0:T(8,128)(2,1)}, bf16[16,1024,128]{2,1,0:T(8,128)(2,1)}, u32[]{:S(2)}, u32[]{:S(2)}) collective-permute-start(bf16[16,1024,128]{2,1,0:T(8,128)(2,1)} %get-tuple-element.9.half_hbm), channel_id=1, source_target_pairs={{0,1},{1,0},{2,3},{3,2},{4,5},{5,4},{6,7},{7,6},{8,9},{9,8},{10,11... | collective-permute-start | bytes 12582920 | tf_op jit(solution)/shard_map/ppermute | solution.py:24
